TPU v7x, 32 devices: a whole 2x2x4 slice. The times are simulated.
32 devices in a mesh: bx: 8 (over y, x, core), by: 4 (over z).
Axes of the slice: x: 2, y: 2, z: 4, core: 2. Of those that a mesh axis runs over, the one named last changes fastest.
Arguments:
- basis: float32 [4, 16, 8, 16, 512], P(None, 'bx', 'by'), may hold values from -6 to 6
- coef: float32 [16, 8, 16], P('bx', 'by'), may hold values from 0.5 to 4
- modes: float32 [3, 8, 8], replicated, may hold values from -1 to 1, as said below
- eigen: float32 [3, 8], replicated, may hold values from 0.2 to 20
- mask: int32 [16, 8, 16], P('bx', 'by'), may hold values 0 or 1
- vertex_ids: int32 [8, 4, 2, 2, 4], P('bx', 'by'), may hold values from 0 to 127, as said below
- coarse_inverse: float32 [128, 128], P('bx'), as said below
Outputs:
- precond: float32 [16, 8, 16, 512], P('bx', 'by')
- next_vector: float32 [16, 8, 16, 512], P('bx', 'by')
- hessen: float32 [5], replicated
Inputs may be any that keep to these rules, and one draw needn't show every extreme that they name: `modes`: each of the three matrices is orthogonal. `vertex_ids`: entry [p, q, a, b, l] is the number of the coarse vertex at corner (p + a, q + b) of the brick grid, taken with wraparound, on level l along the third dimension; bricks beside one another share their corner vertices, and every number is used. `coarse_inverse`: symmetric and positive definite.
All inputs are finite; a program needn't handle non-finite values. No bound on the sum of `mask` on one device may be relied on, other than what follows from the above.
Results may differ from a plain program's by a relative error of at most 0.0022.
Values sent between devices are 32-bit elements; how exact they have to be, the bound alone decides.
No kernel may reach another device: no remote copies, remote signals or barrier semaphores. Data moves between devices by JAX's collectives and lax.ppermute only.
A program may use at most 128 MiB of HBM per device.

v0:
```python
import functools
import math

import jax
import jax.numpy as jnp
from jax import lax
from jax.experimental import pallas as pl
from jax.experimental.pallas import tpu as pltpu
from jax.sharding import PartitionSpec as P


PTS = 8
NODES = PTS**3
KV = 4
CGZ = 4
EX = 2
EY = 2
EZ = 16
LANES = 128
VMEM_BYTES = 12 << 20
HALF = 8
XY = 4 * EX * EY
VERTS = 4 * CGZ

PENALTY = 2.0
SHIFT = 1.0
EPSILON = 1e-06
HIGHEST = lax.Precision.HIGHEST
F32 = jnp.float32
BF16 = jnp.bfloat16


def lane_ids(rows, lanes):
    return lax.broadcasted_iota(jnp.int32, (rows, lanes), 1)


def row_ids(rows, lanes):
    return lax.broadcasted_iota(jnp.int32, (rows, lanes), 0)


def roll_chunks(x, shift):
    shift = shift % LANES
    if shift == 0:
        return x
    pieces = [
        pltpu.roll(x[:, c : c + LANES], shift, 1) for c in range(0, x.shape[1], LANES)
    ]
    return pieces[0] if len(pieces) == 1 else jnp.concatenate(pieces, axis=1)


def column(row):
    wide = jnp.broadcast_to(row, (EZ, EZ))
    keep = row_ids(EZ, EZ) == lane_ids(EZ, EZ)
    return jnp.sum(jnp.where(keep, wide, jnp.zeros_like(wide)), axis=1, keepdims=True)


def columns(ref):
    return [[column(ref[x, y : y + 1, :].astype(F32)) for y in range(EY)] for x in range(EX)]


def blocks_of(parts):
    return [part[8 * b : 8 * b + 8] for part in parts for b in range(EZ // 8)]


def pack_x(parts, high):
    low_half = lane_ids(8, LANES) < 64
    offset = NODES - LANES if high else 0
    cut = [block[:, offset : offset + LANES] for block in blocks_of(parts)]
    out = []
    for m in range(2):
        even = pltpu.roll(cut[2 * m], 64, 1) if high else cut[2 * m]
        odd = cut[2 * m + 1] if high else pltpu.roll(cut[2 * m + 1], 64, 1)
        out.append(jnp.where(low_half, even, odd))
    return jnp.concatenate(out, axis=1)


def unpack_x(packed, high):
    low_half = lane_ids(8, LANES) < 64
    zero = jnp.zeros((8, LANES), F32)
    groups = []
    for g in range(2):
        rows = []
        for b in (2 * g, 2 * g + 1):
            chunk = packed[:, LANES * (b // 2) : LANES * (b // 2) + LANES]
            if (b % 2 == 0) == high:
                chunk = pltpu.roll(chunk, 64, 1)
            chunk = jnp.where(low_half, zero, chunk) if high else jnp.where(low_half, chunk, zero)
            rows.append(
                jnp.concatenate([zero] * 3 + [chunk] if high else [chunk] + [zero] * 3, axis=1)
            )
        groups.append(jnp.concatenate(rows, axis=0))
    return groups


def pack_y(parts, high):
    slot = lane_ids(8, NODES) // PTS % PTS
    from_slot = PTS - 1 if high else 0
    total = jnp.zeros((8, NODES), F32)
    for b, block in enumerate(blocks_of(parts)):
        total = jnp.where(slot == b, roll_chunks(block, PTS * (b - from_slot)), total)
    lower, upper = total[:, :256], roll_chunks(total[:, 256:], 32)
    return jnp.where(slot[:, :256] < 4, lower, upper)


def unpack_y(packed, high):
    slot = lane_ids(8, LANES) // PTS % PTS
    to_slot = PTS - 1 if high else 0
    zero = jnp.zeros((8, LANES), F32)
    groups = []
    for g in range(2):
        rows = []
        for b in (2 * g, 2 * g + 1):
            chunks = []
            for c in range(4):
                source = packed[:, LANES * (c % 2) : LANES * (c % 2) + LANES]
                moved = roll_chunks(source, PTS * (to_slot - b - 4 * (c // 2)))
                chunks.append(jnp.where(slot == to_slot, moved, zero))
            rows.append(jnp.concatenate(chunks, axis=1))
        groups.append(jnp.concatenate(rows, axis=0))
    return groups


def pack_all(groups):
    return [
        pack_x([groups[EX - 1][y] for y in range(EY)], True),
        pack_x([groups[0][y] for y in range(EY)], False),
        pack_y([groups[x][EY - 1] for x in range(EX)], True),
        pack_y([groups[x][0] for x in range(EX)], False),
    ]


def unpack_all(packed):
    left = unpack_x(packed[0], False)
    right = unpack_x(packed[1], True)
    front = unpack_y(packed[2], False)
    back = unpack_y(packed[3], True)
    out = [[None] * EY for _ in range(EX)]
    for x in range(EX):
        for y in range(EY):
            terms = []
            if x == 0:
                terms.append(left[y])
            if x == EX - 1:
                terms.append(right[y])
            if y == 0:
                terms.append(front[x])
            if y == EY - 1:
                terms.append(back[x])
            out[x][y] = functools.reduce(jnp.add, terms)
    return out


def own_neighbors(groups):
    lane = lane_ids(EZ, NODES)
    row = row_ids(EZ, NODES)
    j, k = lane // PTS % PTS, lane % PTS
    low_z = jnp.logical_and(k == 0, row > 0)
    high_z = jnp.logical_and(k == PTS - 1, row < EZ - 1)
    zero = jnp.zeros((EZ, NODES), F32)
    pad = jnp.zeros((EZ, NODES - LANES), F32)
    low_half = lane_ids(EZ, LANES) < 64
    zero_chunk = jnp.zeros((EZ, LANES), F32)
    out = [[None] * EY for _ in range(EX)]
    for x in range(EX):
        for y in range(EY):
            here = groups[x][y]
            total = jnp.where(low_z, roll_chunks(pltpu.roll(here, 1, 0), 1 - PTS), zero)
            total = total + jnp.where(
                high_z, roll_chunks(pltpu.roll(here, EZ - 1, 0), PTS - 1), zero
            )
            if y > 0:
                moved = roll_chunks(groups[x][y - 1], PTS - PTS * PTS)
                total = total + jnp.where(j == 0, moved, zero)
            if y < EY - 1:
                moved = roll_chunks(groups[x][y + 1], PTS * PTS - PTS)
                total = total + jnp.where(j == PTS - 1, moved, zero)
            if x > 0:
                chunk = pltpu.roll(groups[x - 1][y][:, NODES - LANES :], 64, 1)
                chunk = jnp.where(low_half, chunk, zero_chunk)
                total = total + jnp.concatenate([chunk, pad], axis=1)
            if x < EX - 1:
                chunk = pltpu.roll(groups[x + 1][y][:, :LANES], 64, 1)
                chunk = jnp.where(low_half, zero_chunk, chunk)
                total = total + jnp.concatenate([pad, chunk], axis=1)
            out[x][y] = total
    return out


def load_groups(ref, *lead):
    return [[ref[(*lead, x, y)] for y in range(EY)] for x in range(EX)]


def stack(groups):
    return jnp.concatenate([groups[x][y] for x in range(EX) for y in range(EY)], axis=0)


def unstack(whole):
    return [
        [whole[(x * EY + y) * EZ : (x * EY + y + 1) * EZ] for y in range(EY)] for x in range(EX)
    ]


def hat(place, span, levels, level):
    place = place.astype(F32) / float(span) * float(levels - 1)
    return jnp.maximum(0.0, 1.0 - jnp.abs(place - float(level)))


def hat_z():
    lane, row = lane_ids(EZ, NODES), row_ids(EZ, NODES)
    place = row * (PTS - 1) + lane % PTS
    return [hat(place, EZ * (PTS - 1), CGZ, level) for level in range(CGZ)]


def hat_x(x, a, rows=1):
    place = x * (PTS - 1) + lane_ids(rows, NODES) // (PTS * PTS)
    return hat(place, EX * (PTS - 1), 2, a)


def hat_y(y, b, rows=1):
    place = y * (PTS - 1) + lane_ids(rows, NODES) // PTS % PTS
    return hat(place, EY * (PTS - 1), 2, b)


def face_count(rows):
    lane = lane_ids(rows, NODES)
    total = jnp.zeros((rows, NODES), F32)
    for part in (lane // (PTS * PTS), lane // PTS % PTS, lane % PTS):
        edge = jnp.logical_or(part == 0, part == PTS - 1)
        total = total + jnp.where(edge, 1.0, 0.0)
    return total


def all_sum(x):
    return jnp.sum(jnp.sum(x, axis=0, keepdims=True), axis=1, keepdims=True)


def coarse_row(current, ids_ref, count, scale):
    weight_z = hat_z()
    lane = lane_ids(1, count)
    out = jnp.zeros((1, count), F32)
    for level in range(CGZ):
        sums = [[None] * EY for _ in range(EX)]
        for x in range(EX):
            for y in range(EY):
                sums[x][y] = jnp.sum(current[x][y] * weight_z[level], axis=0, keepdims=True)
        for a in range(2):
            for b in range(2):
                total = jnp.zeros((1, NODES), F32)
                for x in range(EX):
                    for y in range(EY):
                        total = total + sums[x][y] * (hat_x(x, a) * hat_y(y, b))
                value = jnp.sum(total, axis=1, keepdims=True) * scale
                out = out + jnp.where(lane == ids_ref[0, 0, a, b, level], value, 0.0)
    return out


def send_faces(basis_ref, mask_ref, outs):
    current = load_groups(basis_ref, KV - 1)
    active = columns(mask_ref)
    wide = [[jnp.broadcast_to(active[x][y], (EZ, NODES)) for y in range(EY)] for x in range(EX)]
    for ref, face, part in zip(outs, pack_all(current), pack_all(wide)):
        ref[0:8, :] = face
        ref[8:16, :] = part
    return current


def start_kernel(scale, count, basis_ref, mask_ref, ids_ref, row_ref, *outs):
    current = send_faces(basis_ref, mask_ref, outs)
    row_ref[...] = coarse_row(current, ids_ref, count, scale)


def load_kernel(*refs):
    basis_hbm, mask_hbm, coef_hbm, modes_hbm, eigen_hbm, ids_hbm, inverse_hbm = refs[:7]
    basis_ref, mask_ref, coef_ref, modes_ref, eigen_ref, inverse_ref, ids_ref = refs[7:14]
    outs, ids_scratch, sems = refs[14:18], refs[18], refs[19]
    older = slice(0, KV - 1)
    copies = [
        pltpu.make_async_copy(source, target, sems.at[n])
        for n, (source, target) in enumerate(
            (
                (basis_hbm.at[KV - 1], basis_ref.at[KV - 1]),
                (mask_hbm, mask_ref),
                (basis_hbm.at[older], basis_ref.at[older]),
                (coef_hbm, coef_ref),
                (modes_hbm, modes_ref),
                (eigen_hbm, eigen_ref),
                (ids_hbm, ids_scratch),
                (inverse_hbm, inverse_ref),
            )
        )
    ]
    for copy in copies:
        copy.start()
    copies[0].wait()
    copies[1].wait()
    send_faces(basis_ref, mask_ref, outs)
    for copy in copies[2:]:
        copy.wait()
    lane = lane_ids(1, LANES)
    row = jnp.zeros((1, LANES), F32)
    for a in range(2):
        for b in range(2):
            short = ids_scratch[0, 0, a, b : b + 1, :].astype(F32)
            for level in range(CGZ):
                row = jnp.where(lane == 80 + (a * 2 + b) * CGZ + level, short[:, level : level + 1], row)
    ids_ref[...] = jnp.broadcast_to(row, (8, LANES))


def expand(matrix, stride):
    pick = (lane_ids(PTS, NODES) // stride % PTS == row_ids(PTS, NODES)).astype(F32)
    return jnp.dot(matrix, pick, precision=HIGHEST, preferred_element_type=F32)


def tables_kernel(modes_ref, eigen_ref, sb_ref, st_ref, lh_ref, ll_ref, xy_ref, z_ref):
    strides = (PTS * PTS, PTS, 1)
    eye = (row_ids(PTS, PTS) == lane_ids(PTS, PTS)).astype(F32)
    straight, turned, stiff, unit = [], [], [], []
    for d in range(3):
        mode = modes_ref[d]
        turn = lax.dot_general(
            mode, eye, (((0,), (0,)), ((), ())), precision=HIGHEST, preferred_element_type=F32
        )
        scaled = mode * eigen_ref[d : d + 1, :]
        one = jnp.dot(scaled, turn, precision=HIGHEST, preferred_element_type=F32)
        straight.append(expand(mode, strides[d]))
        turned.append(expand(turn, strides[d]))
        stiff.append(expand(one, strides[d]))
        unit.append(expand(eye, strides[d]))
    for i in range(PTS):
        for j in range(PTS):
            rows = slice((i * PTS + j) * PTS, (i * PTS + j + 1) * PTS)
            pair = straight[0][i : i + 1] * straight[1][j : j + 1]
            sb_ref[rows, :] = (pair * straight[2]).astype(BF16)
            pair = turned[0][i : i + 1] * turned[1][j : j + 1]
            st_ref[rows, :] = (pair * turned[2]).astype(BF16)
            both = unit[0][i : i + 1] * unit[1][j : j + 1]
            either = stiff[0][i : i + 1] * unit[1][j : j + 1] + unit[0][i : i + 1] * stiff[1][j : j + 1]
            full = either * unit[2] + both * stiff[2]
            head = full.astype(BF16)
            lh_ref[rows, :] = head
            ll_ref[rows, :] = (full - head.astype(F32)).astype(BF16)
    point, row = lane_ids(PTS, PTS), row_ids(PTS, PTS)
    pairs = (row < 2 * EX, row // 2 * (PTS - 1) + point, row % 2)
    short = jnp.maximum(
        0.0,
        1.0 - jnp.abs(pairs[1].astype(F32) / float(EX * (PTS - 1)) - pairs[2].astype(F32)),
    )
    short = jnp.where(pairs[0], short, 0.0)
    stiff_x = jnp.dot(short, stiff[0], precision=HIGHEST, preferred_element_type=F32)
    stiff_y = jnp.dot(short, stiff[1], precision=HIGHEST, preferred_element_type=F32)
    for a in range(2):
        for b in range(2):
            for x in range(EX):
                for y in range(EY):
                    at = ((a * 2 + b) * EX + x) * EY + y
                    plain_x, plain_y = hat_x(x, a), hat_y(y, b)
                    xy_ref[at : at + 1, :] = plain_x * plain_y
                    xy_ref[XY + at : XY + at + 1, :] = (
                        stiff_x[x * 2 + a : x * 2 + a + 1] * plain_y
                        + plain_x * stiff_y[y * 2 + b : y * 2 + b + 1]
                    )
    place = row_ids(EZ, PTS) * (PTS - 1) + lane_ids(EZ, PTS)
    for level, weight in enumerate(hat_z()):
        z_ref[level * EZ : (level + 1) * EZ, :] = weight
        tall = hat(place, EZ * (PTS - 1), CGZ, level)
        z_ref[(CGZ + level) * EZ : (CGZ + level + 1) * EZ, :] = jnp.dot(
            tall, stiff[2], precision=HIGHEST, preferred_element_type=F32
        )


def spectrum_row(eigen_ref):
    out = jnp.zeros((1, NODES), F32)
    for d, stride in enumerate((PTS * PTS, PTS, 1)):
        pick = (lane_ids(PTS, NODES) // stride % PTS == row_ids(PTS, NODES)).astype(F32)
        out = out + jnp.dot(
            eigen_ref[d : d + 1, :], pick, precision=HIGHEST, preferred_element_type=F32
        )
    return out


def smooth_kernel(*refs):
    basis_ref, coef_ref, mask_ref, eigen_ref, sb_ref, st_ref = refs[:6]
    halo = [ref[0:8, :] for ref in refs[6:10]]
    smooth_ref, *send = refs[10:]
    current = load_groups(basis_ref, KV - 1)
    inside, outside = own_neighbors(current), unpack_all(halo)
    coef, active = columns(coef_ref), columns(mask_ref)
    extended = [
        [current[x][y] + (inside[x][y] + outside[x][y]) for y in range(EY)] for x in range(EX)
    ]
    modal = jnp.dot(stack(extended).astype(BF16), sb_ref[...], preferred_element_type=F32)
    modal = unstack(modal)
    spectrum = spectrum_row(eigen_ref)
    modal = [
        [modal[x][y] / (coef[x][y] * spectrum + SHIFT) for y in range(EY)] for x in range(EX)
    ]
    smooth = jnp.dot(stack(modal).astype(BF16), st_ref[...], preferred_element_type=F32)
    smooth = unstack(smooth)
    smooth = [[smooth[x][y] * active[x][y] for y in range(EY)] for x in range(EX)]
    for x in range(EX):
        for y in range(EY):
            smooth_ref[x, y] = smooth[x][y]
    for ref, face in zip(send, pack_all(smooth)):
        ref[...] = face


def stiff_apply(groups, lh_ref, ll_ref):
    whole = stack(groups)
    head = whole.astype(BF16)
    tail = (whole - head.astype(F32)).astype(BF16)
    rows = whole.shape[0]
    both = jnp.dot(jnp.concatenate([head, tail], axis=0), lh_ref[...], preferred_element_type=F32)
    low = jnp.dot(head, ll_ref[...], preferred_element_type=F32)
    return unstack(both[:rows] + (both[rows:] + low))


def image_kernel(count, *refs):
    basis_ref, smooth_ref, coef_ref, mask_ref, ids_ref, got_ref, lh_ref, ll_ref = refs[:8]
    face_refs, mask_refs = refs[8:12], refs[12:16]
    precond_ref, image_ref, row_ref = refs[16:]
    coef, active = columns(coef_ref), columns(mask_ref)
    solved = got_ref[...]
    lane = lane_ids(1, count)
    weight_z = hat_z()
    field = [[jnp.zeros((EZ, NODES), F32) for _ in range(EY)] for _ in range(EX)]
    for a in range(2):
        for b in range(2):
            along = jnp.zeros((EZ, NODES), F32)
            for level in range(CGZ):
                hit = jnp.where(lane == ids_ref[0, 0, a, b, level], solved, 0.0)
                along = along + weight_z[level] * jnp.sum(hit, axis=1, keepdims=True)
            for x in range(EX):
                for y in range(EY):
                    field[x][y] = field[x][y] + along * (hat_x(x, a) * hat_y(y, b))
    smooth = load_groups(smooth_ref)
    precond = [
        [smooth[x][y] + active[x][y] * field[x][y] for y in range(EY)] for x in range(EX)
    ]
    stiff = stiff_apply(precond, lh_ref, ll_ref)
    inside = own_neighbors(precond)
    outside = unpack_all([ref[...] for ref in face_refs])
    open_faces = unpack_all([ref[8:16, :] for ref in mask_refs])
    counts = face_count(EZ)
    dots = [jnp.zeros((EZ, NODES), F32) for _ in range(KV + 1)]
    for x in range(EX):
        for y in range(EY):
            across = outside[x][y] + open_faces[x][y] * field[x][y]
            image = active[x][y] * (
                coef[x][y] * stiff[x][y]
                + PENALTY * (counts * precond[x][y] - (inside[x][y] + across))
            )
            precond_ref[x, y] = precond[x][y]
            image_ref[x, y] = image
            for v in range(KV):
                dots[v] = dots[v] + basis_ref[v, x, y] * image
            dots[KV] = dots[KV] + image * image
    values = [all_sum(d) for d in dots]
    basis = [load_groups(basis_ref, v) for v in range(KV)]
    for v in range(KV):
        for u in range(v, KV):
            total = jnp.zeros((EZ, NODES), F32)
            for x in range(EX):
                for y in range(EY):
                    total = total + basis[v][x][y] * basis[u][x][y]
            values.append(all_sum(total))
    row = jnp.zeros((1, LANES), F32)
    row_lane = lane_ids(1, LANES)
    for position, value in enumerate(values):
        row = jnp.where(row_lane == position, value, row)
    row_ref[...] = row


def finish_kernel(total_points, basis_ref, image_ref, got_ref, next_ref, hessen_ref):
    sums = got_ref[...] / total_points
    lane = lane_ids(1, LANES)

    def pick(position):
        return jnp.sum(jnp.where(lane == position, sums, 0.0), axis=1, keepdims=True)

    proj = [pick(v) for v in range(KV)]
    square = pick(KV)
    position = KV + 1
    quad = jnp.zeros((1, 1), F32)
    for v in range(KV):
        for u in range(v, KV):
            factor = 1.0 if u == v else 2.0
            quad = quad + factor * proj[v] * proj[u] * pick(position)
            position += 1
    dot = functools.reduce(jnp.add, [p * p for p in proj])
    beta = jnp.sqrt(square - 2.0 * dot + quad + EPSILON)
    for x in range(EX):
        for y in range(EY):
            residual = image_ref[x, y]
            for v in range(KV):
                residual = residual - proj[v] * basis_ref[v, x, y]
            next_ref[x, y] = residual / beta
    for v, value in enumerate(proj + [beta]):
        hessen_ref[v] = jnp.sum(value)


def levels_of(half):
    found = []
    for level in range(CGZ):
        for point in range(half * HALF * (PTS - 1), (half * HALF + HALF - 1) * (PTS - 1) + PTS):
            if abs(point * (CGZ - 1) / (EZ * (PTS - 1)) - level) < 1.0 + 1e-3:
                found.append(level)
                break
    return found


def lane_sums(x):
    return lax.dot_general(
        jnp.ones((8, LANES), F32),
        x,
        (((1,), (1,)), ((), ())),
        precision=HIGHEST,
        preferred_element_type=F32,
    )


def fold(acc):
    return jnp.sum(acc, axis=0, keepdims=True)


def pieces_of(half):
    for x in range(EX):
        for y in range(EY):
            for c in range(NODES // LANES):
                yield x, y, slice(half * HALF, half * HALF + HALF), slice(c * LANES, (c + 1) * LANES)


def products(left, right, halves, out_row):
    accs = {}
    for half in halves:
        lefts, rights = left(half), right(half)
        for piece in pieces_of(half):
            own = {v: load(*piece) for v, load in lefts.items()}
            other = own if rights is None else {w: load(*piece) for w, load in rights.items()}
            for v, first in own.items():
                for w, second in other.items():
                    if rights is None and w < v:
                        continue
                    term = first * second
                    accs[v, w] = accs[v, w] + term if (v, w) in accs else term
    for (v, w), acc in accs.items():
        out_row(v, w, fold(acc))


def fields_kernel(scale, basis_ref, coef_ref, mask_ref, *refs):
    mask_refs, (xy_ref, z_ref) = refs[:4], refs[4:6]
    early_ref, field_ref, wall_ref, rows_ref = refs[6:]
    coef, active = columns(coef_ref), columns(mask_ref)
    wide = [[jnp.broadcast_to(active[x][y], (EZ, NODES)) for y in range(EY)] for x in range(EX)]
    inside, outside = own_neighbors(wide), unpack_all([ref[8:16, :] for ref in mask_refs])
    counts = face_count(EZ)
    halves = range(EZ // HALF)
    levels = [levels_of(half) for half in halves]
    for x in range(EX):
        for y in range(EY):
            wall = active[x][y] * PENALTY * (counts - (inside[x][y] + outside[x][y]))
            wall_ref[x, y] = wall
            weight = active[x][y] * coef[x][y]
            for half in halves:
                rows = slice(half * HALF, half * HALF + HALF)
                for ab in range(4):
                    at = (ab * EX + x) * EY + y
                    plain = xy_ref[at : at + 1, :]
                    first = weight[rows] * xy_ref[XY + at : XY + at + 1, :] + wall[rows] * plain
                    second = weight[rows] * plain
                    for level in levels[half]:
                        tall = slice(level * EZ + half * HALF, level * EZ + half * HALF + HALF)
                        stiff = slice((CGZ + level) * EZ + half * HALF, (CGZ + level) * EZ + half * HALF + HALF)
                        field_ref[ab * CGZ + level, x, y, rows, :] = (
                            z_ref[tall, :] * first + z_ref[stiff, :] * second
                        )
    rows_ref[...] = jnp.zeros_like(rows_ref)

    def fields(ab):
        def at(half):
            return {
                ab * CGZ + level: (lambda x, y, r, c, v=ab * CGZ + level: field_ref[v, x, y, r, c])
                for level in levels[half]
            }

        return at

    def vectors(half):
        return {v: (lambda x, y, r, c, v=v: basis_ref[v, x, y, r, c]) for v in range(KV)}

    def put(row, value):
        rows_ref[row : row + 1, :] = value

    position = {}
    for v in range(KV):
        for u in range(v, KV):
            position[v, u] = len(position)
    products(vectors, lambda half: None, halves, lambda v, u, s: put(96 + position[v, u], s))
    for ab in range(4):
        products(vectors, fields(ab), halves, lambda v, w, s: put(v * VERTS + w, s))
        products(fields(ab), lambda half: None, halves, lambda v, w, s: put(LANES + v * VERTS + w, s))
        for other in range(ab + 1, 4):
            products(fields(ab), fields(other), halves, lambda v, w, s: put(LANES + v * VERTS + w, s))
    for level in range(CGZ):
        sums = [[None] * EY for _ in range(EX)]
        for x in range(EX):
            for y in range(EY):
                sums[x][y] = fold(basis_ref[KV - 1, x, y] * z_ref[level * EZ : (level + 1) * EZ, :])
        for ab in range(4):
            total = jnp.zeros((1, NODES), F32)
            for x in range(EX):
                for y in range(EY):
                    at = (ab * EX + x) * EY + y
                    total = total + sums[x][y] * xy_ref[at : at + 1, :]
            parts = [total[:, c : c + LANES] for c in range(0, NODES, LANES)]
            put(64 + ab * CGZ + level, functools.reduce(jnp.add, parts) * scale)
    early_ref[...] = lane_sums(rows_ref[...])


def base_kernel(rows, peers, *refs):
    basis_ref, smooth_ref, coef_ref, mask_ref, ids_ref, inverse_ref, lh_ref, ll_ref = refs[:8]
    face_refs, early_ref, field_ref = refs[8:12], refs[12], refs[13]
    base_ref, send_ref, rows_ref = refs[14:]
    coef, active = columns(coef_ref), columns(mask_ref)
    smooth = load_groups(smooth_ref)
    stiff = stiff_apply(smooth, lh_ref, ll_ref)
    inside = own_neighbors(smooth)
    outside = unpack_all([ref[...] for ref in face_refs])
    counts = face_count(EZ)
    for x in range(EX):
        for y in range(EY):
            base_ref[x, y] = active[x][y] * (
                coef[x][y] * stiff[x][y]
                + PENALTY * (counts * smooth[x][y] - (inside[x][y] + outside[x][y]))
            )
    rows_ref[...] = jnp.zeros_like(rows_ref)
    halves = range(EZ // HALF)

    def base(half):
        return {KV: (lambda x, y, r, c: base_ref[x, y, r, c])}

    def vectors(half):
        found = {v: (lambda x, y, r, c, v=v: basis_ref[v, x, y, r, c]) for v in range(KV)}
        found.update(base(half))
        return found

    def fields(part):
        def at(half):
            return {
                v: (lambda x, y, r, c, v=v: field_ref[v, x, y, r, c])
                for v in range(part * 8, part * 8 + 8)
                if v % CGZ in levels_of(half)
            }

        return at

    def put(row, value):
        rows_ref[row : row + 1, :] = value

    products(base, vectors, halves, lambda v, w, s: put(w, s))
    for part in range(VERTS // 8):
        products(base, fields(part), halves, lambda v, w, s: put(VERTS + w, s))
    late = lane_sums(rows_ref[...])
    lane, row = lane_ids(8, LANES), row_ids(8, LANES)
    early = early_ref[...]
    tile = early[:, :LANES]
    tile = jnp.where(jnp.logical_and(lane >= 80, lane < 80 + VERTS), ids_ref[...], tile)
    tile = jnp.where(row == 1, early[:, LANES : 2 * LANES], tile)
    tile = jnp.where(row == 2, early[:, 2 * LANES :], tile)
    tile = jnp.where(row == 3, late, tile)
    first = lax.axis_index("by") * rows
    for r in range(rows):
        tile = jnp.where(row == 4 + r, inverse_ref[pl.ds(first + r, 1), :], tile)
    for peer in range(peers):
        send_ref[8 * peer : 8 * peer + 8, :] = tile


def close_kernel(total_points, rows, peers, *refs):
    basis_ref, smooth_ref, base_ref, wall_ref, coef_ref, mask_ref, ids_ref = refs[:7]
    xy_ref, z_ref, got_ref, precond_ref, next_ref, hessen_ref = refs[7:]
    lane, row = lane_ids(peers, LANES), row_ids(peers, LANES)

    def got(r):
        return got_ref[pl.ds(r, peers, stride=8), :]

    sums, late = got(0), got(3)
    number = lane.astype(F32)
    hits = [number == sums[:, 80 + v : 81 + v] for v in range(VERTS)]
    coarse = jnp.zeros((peers, LANES), F32)
    for v in range(VERTS):
        coarse = coarse + jnp.where(hits[v], sums[:, 64 + v : 65 + v], 0.0)
    coarse = fold(coarse)
    solved = jnp.zeros((peers, LANES), F32)
    for r in range(rows):
        part = jnp.where(lane == row * rows + r, coarse, 0.0)
        solved = solved + jnp.sum(part, axis=1, keepdims=True) * got(4 + r)
    solved = fold(solved)
    spread = jnp.zeros((peers, LANES), F32)
    wide = [jnp.zeros((peers, LANES), F32) for _ in range(2)]
    for v in range(VERTS):
        value = jnp.sum(jnp.where(hits[v], solved, 0.0), axis=1, keepdims=True)
        spread = jnp.where(lane % VERTS == v, value, spread)
        part = v * VERTS // LANES
        wide[part] = jnp.where(lane // VERTS == v - part * 8, value, wide[part])
    upper = [lane % VERTS > lane // VERTS + part * 8 for part in range(2)]
    twice = [jnp.where(u, 2.0, 1.0) for u in upper]
    quad = (got(1) * wide[0] * twice[0] + got(2) * wide[1] * twice[1]) * spread
    linear = fold(sums * spread)
    late_sum = fold(late)
    in_g = jnp.logical_and(lane >= VERTS, lane < 2 * VERTS)
    square = quad + jnp.where(in_g, 2.0 * late * spread, 0.0) + jnp.where(lane == KV, late, 0.0)
    square = jnp.sum(fold(square), axis=1, keepdims=True) / total_points
    line = lane_ids(1, LANES)
    proj = []
    for v in range(KV):
        term = jnp.where(line // VERTS == v, linear, 0.0) + jnp.where(line == v, late_sum, 0.0)
        proj.append(jnp.sum(term, axis=1, keepdims=True) / total_points)
    pair = jnp.zeros((1, LANES), F32)
    position = 96
    for v in range(KV):
        for u in range(v, KV):
            factor = 1.0 if u == v else 2.0
            pair = jnp.where(line == position, factor * proj[v] * proj[u], pair)
            position += 1
    gram = jnp.sum(pair * fold(sums), axis=1, keepdims=True) / total_points
    dot = functools.reduce(jnp.add, [p * p for p in proj])
    beta = jnp.sqrt(square - 2.0 * dot + gram + EPSILON)
    coef, active = columns(coef_ref), columns(mask_ref)
    along, bent = [], []
    for a in range(2):
        for b in range(2):
            plain = jnp.zeros((EZ, NODES), F32)
            stiff = jnp.zeros((EZ, NODES), F32)
            for level in range(CGZ):
                at = 80 + (a * 2 + b) * CGZ + level
                hit = jnp.where(line.astype(F32) == ids_ref[0:1, at : at + 1], solved, 0.0)
                value = jnp.sum(hit, axis=1, keepdims=True)
                plain = plain + value * z_ref[level * EZ : (level + 1) * EZ, :]
                stiff = stiff + value * z_ref[(CGZ + level) * EZ : (CGZ + level + 1) * EZ, :]
            along.append(plain)
            bent.append(stiff)
    for x in range(EX):
        for y in range(EY):
            field = jnp.zeros((EZ, NODES), F32)
            image = jnp.zeros((EZ, NODES), F32)
            for ab in range(4):
                at = (ab * EX + x) * EY + y
                plain = xy_ref[at : at + 1, :]
                field = field + along[ab] * plain
                image = image + (along[ab] * xy_ref[XY + at : XY + at + 1, :] + bent[ab] * plain)
            precond_ref[x, y] = smooth_ref[x, y] + active[x][y] * field
            residual = (
                base_ref[x, y] + (active[x][y] * coef[x][y]) * image + wall_ref[x, y] * field
            )
            for v in range(KV):
                residual = residual - proj[v] * basis_ref[v, x, y]
            next_ref[x, y] = residual / beta
    for v, value in enumerate(proj + [beta]):
        hessen_ref[v] = jnp.sum(value)


def spec(kind=pltpu.VMEM):
    return pl.BlockSpec(memory_space=kind)


def call(kernel, outs, in_specs, args, out_specs=None, scratch=(), cost=1000000):
    return pl.pallas_call(
        kernel,
        out_shape=[jax.ShapeDtypeStruct(shape, dtype) for shape, dtype in outs],
        in_specs=in_specs,
        out_specs=out_specs or [spec() for _ in outs],
        scratch_shapes=scratch,
        compiler_params=pltpu.CompilerParams(vmem_limit_bytes=VMEM_BYTES),
        cost_estimate=pl.CostEstimate(flops=cost, bytes_accessed=cost, transcendentals=0),
    )(*args)


def exchange(sends):
    out = [None] * 4
    for place in (3, 2, 1, 0):
        axis = "bx" if place < 2 else "by"
        size = lax.axis_size(axis)
        ring = [(i, (i + 1) % size) for i in range(size)]
        if place % 2:
            ring = [(j, i) for i, j in ring]
        out[place] = lax.ppermute(sends[place], axis, ring)
    return out


def smooth_part(basis, coef, modes, eigen, mask, sends):
    halo = exchange(sends)
    square = ((NODES, NODES), BF16)
    tables = call(
        tables_kernel,
        [square] * 4 + [((2 * XY, NODES), F32), ((2 * CGZ * EZ, NODES), F32)],
        [spec()] * 2,
        (modes, eigen),
    )
    smooth, *sends = call(
        smooth_kernel,
        [FIELD] + [((8, 256), F32)] * 4,
        [spec()] * 10,
        (basis, coef, mask, eigen, tables[0], tables[1], *halo),
    )
    return halo, tables, smooth, exchange(sends)


FIELD = ((EX, EY, EZ, NODES), F32)
SENDS = [((16, 256), F32)] * 4


def one_exchange(basis, coef, modes, eigen, mask, vertex_ids, coarse_inverse):
    peers = lax.axis_size("bx") * lax.axis_size("by")
    rows = coarse_inverse.shape[1] // peers
    points = EX * EY * EZ * NODES
    *local, a, b, c, d = call(
        load_kernel,
        [(x.shape, x.dtype) for x in (basis, mask, coef, modes, eigen, coarse_inverse)]
        + [((8, LANES), F32)]
        + SENDS,
        [spec(pltpu.HBM)] * 7,
        tuple(pltpu.with_memory_space_constraint(x, pltpu.HBM) for x in (basis, mask, coef, modes, eigen, vertex_ids, coarse_inverse)),
        scratch=[pltpu.VMEM(vertex_ids.shape, vertex_ids.dtype), pltpu.SemaphoreType.DMA((8,))],
    )
    basis, mask, coef, modes, eigen, coarse_inverse, ids = local
    halo, tables, smooth, faces = smooth_part(basis, coef, modes, eigen, mask, (a, b, c, d))
    early, fields, wall = call(
        functools.partial(fields_kernel, 1.0 / math.sqrt(points)),
        [((8, 3 * LANES), F32), ((VERTS,) + FIELD[0], F32), FIELD],
        [spec()] * 9,
        (basis, coef, mask, *halo, tables[4], tables[5]),
        scratch=[pltpu.VMEM((3 * LANES, LANES), F32)],
    )
    base, row = call(
        functools.partial(base_kernel, rows, peers),
        [FIELD, ((8 * peers, LANES), F32)],
        [spec()] * 14,
        (basis, smooth, coef, mask, ids, coarse_inverse, *tables[2:4], *faces, early, fields),
        scratch=[pltpu.VMEM((LANES, LANES), F32)],
    )
    got = lax.all_to_all(row, ("bx", "by"), 0, 0, tiled=True)
    return call(
        functools.partial(close_kernel, float(points * peers), rows, peers),
        [FIELD, FIELD, ((KV + 1,), F32)],
        [spec()] * 10,
        (basis, smooth, base, wall, coef, mask, ids, tables[4], tables[5], got),
        out_specs=[spec(), spec(), spec(pltpu.SMEM)],
    )


def two_exchanges(basis, coef, modes, eigen, mask, vertex_ids, coarse_inverse):
    peers = lax.axis_size("bx") * lax.axis_size("by")
    count = coarse_inverse.shape[1]
    points = EX * EY * EZ * NODES
    row, *sends = call(
        functools.partial(start_kernel, 1.0 / math.sqrt(points), count),
        [((1, count), F32)] + SENDS,
        [spec()] * 2 + [spec(pltpu.SMEM)],
        (basis, mask, vertex_ids),
    )
    coarse = lax.psum(row, ("bx", "by"))
    solved = jnp.dot(coarse_inverse, coarse[0], precision=HIGHEST)
    solved = lax.all_gather(solved, "bx", axis=0, tiled=True)[None]
    halo, tables, smooth, faces = smooth_part(basis, coef, modes, eigen, mask, sends)
    precond, image, row = call(
        functools.partial(image_kernel, count),
        [FIELD, FIELD, ((1, LANES), F32)],
        [spec()] * 4 + [spec(pltpu.SMEM)] + [spec()] * 11,
        (basis, smooth, coef, mask, vertex_ids, solved, tables[2], tables[3], *faces, *halo),
    )
    row = lax.psum(row, ("bx", "by"))
    next_vector, hessen = call(
        functools.partial(finish_kernel, float(points * peers)),
        [FIELD, ((KV + 1,), F32)],
        [spec()] * 3,
        (basis, image, row),
        out_specs=[spec(), spec(pltpu.SMEM)],
    )
    return precond, next_vector, hessen


def body(basis, coef, modes, eigen, mask, vertex_ids, coarse_inverse):
    assert coef.shape == (EX, EY, EZ) and basis.shape[0] == KV
    peers = lax.axis_size("bx") * lax.axis_size("by")
    count = coarse_inverse.shape[1]
    small = count == LANES and count == 4 * peers
    steps = one_exchange if small else two_exchanges
    return tuple(steps(basis, coef, modes, eigen, mask, vertex_ids, coarse_inverse))


def solution(mesh):
    placed = (
        P(None, "bx", "by", None, None),
        P("bx", "by", None),
        P(),
        P(),
        P("bx", "by", None),
        P("bx", "by", None, None, None),
        P("bx", None),
    )
    return jax.shard_map(
        body,
        mesh=mesh,
        in_specs=placed,
        out_specs=(P("bx", "by", None, None), P("bx", "by", None, None), P()),
        check_vma=False,
    )
```

profile of v0, /device:TPU:0, one launch (start us, length us, event | category | flops | bytes accessed | tf_op | source)
XLA Modules:
  0.0 37.1 jit_solution(7252594741379700165)
XLA Ops:
  0.6 1.3 %shard_map.94 = (f32[4,2,2,16,512]{4,3,2,1,0:T(8,128)S(1)}, s32[2,2,16]{2,1,0:T(2,128)S(1)}, f32[2,2,16]{2,1,0:T(2,128)S(1)}, f32[3,8,8]{2,1,0:T(8,128)S(1)}, f3...) custom-call(f32[4,2,2,16,512]{4,3,2,1,0:T(8,128)} %refs_0_.1, ...), custom_call_target="tpu_custom_call" | custom-call | flops 1000000 | bytes 1000000 | tf_op jit(solution)/shard_map/pallas_call | solution.py:766
  2.0 0.5 %collective-permute-start = (f32[16,256]{1,0:T(8,128)S(1)}, f32[16,256]{1,0:T(8,128)S(1)}, u32[]{:S(2)}, u32[]{:S(2)}) collective-permute-start(f32[16,256]{1,0:T(8,128)S(1)} %get-tuple-element.37), channel_id=1, source_target_pairs={{0,4},{4,8},{8,12},{12,16},{16,20},{20,24},{24,28},{28,0},{1,5},{5... | collective-permute-start | bytes 49160 | tf_op jit(solution)/shard_map/ppermute | solution.py:785
  2.5 2.9 %collective-permute-start.1 = (f32[16,256]{1,0:T(8,128)S(1)}, f32[16,256]{1,0:T(8,128)S(1)}, u32[]{:S(2)}, u32[]{:S(2)}) collective-permute-start(f32[16,256]{1,0:T(8,128)S(1)} %get-tuple-element.38), channel_id=1, source_target_pairs={{4,0},{8,4},{12,8},{16,12},{20,16},{24,20},{28,24},{0,28},{5,1},{9... | collective-permute-start | bytes 49160 | tf_op jit(solution)/shard_map/ppermute | solution.py:785
  5.4 2.3 %collective-permute-start.2 = (f32[16,256]{1,0:T(8,128)S(1)}, f32[16,256]{1,0:T(8,128)S(1)}, u32[]{:S(2)}, u32[]{:S(2)}) collective-permute-start(f32[16,256]{1,0:T(8,128)S(1)} %get-tuple-element.39), channel_id=1, source_target_pairs={{0,1},{1,2},{2,3},{3,0},{4,5},{5,6},{6,7},{7,4},{8,9},{9,10},{10,1... | collective-permute-start | bytes 49160 | tf_op jit(solution)/shard_map/ppermute | solution.py:785
  7.7 2.0 %collective-permute-start.3 = (f32[16,256]{1,0:T(8,128)S(1)}, f32[16,256]{1,0:T(8,128)S(1)}, u32[]{:S(2)}, u32[]{:S(2)}) collective-permute-start(f32[16,256]{1,0:T(8,128)S(1)} %get-tuple-element.40), channel_id=1, source_target_pairs={{1,0},{2,1},{3,2},{0,3},{5,4},{6,5},{7,6},{4,7},{9,8},{10,9},{11,1... | collective-permute-start | bytes 49160 | tf_op jit(solution)/shard_map/ppermute | solution.py:785
  9.7 1.9 %shard_map.95 = (bf16[512,512]{1,0:T(8,128)(2,1)S(1)}, bf16[512,512]{1,0:T(8,128)(2,1)S(1)}, bf16[512,512]{1,0:T(8,128)(2,1)S(1)}, bf16[512,512]{1,0:T(8,128)(2,...) custom-call(f32[3,8,8]{2,1,0:T(8,128)S(1)} %get-tuple-element.34.modes_ref, ...), custom_call_target="tpu_custom_call" | custom-call | flops 1000000 | bytes 1000000 | tf_op jit(solution)/shard_map/pallas_call | solution.py:766
  11.6 0.0 collective-permute-done.refs_6_.refs_0_
  11.6 0.0 collective-permute-done.1.refs_7_.refs_1_
  11.7 0.0 collective-permute-done.2.refs_8_.refs_2_
  11.7 0.0 collective-permute-done.3.refs_9_.refs_3_
  11.7 0.7 %shard_map.96 = (f32[2,2,16,512]{3,2,1,0:T(8,128)S(1)}, f32[8,256]{1,0:T(8,128)S(1)}, f32[8,256]{1,0:T(8,128)S(1)}, f32[8,256]{1,0:T(8,128)S(1)}, f32[8,256]{1,0:T(8,128)S(1)}) custom-call(f32[4,2,2,16,512]{4,3,2,1,0:T(8,128)S(1)} %get-tuple-element.30.refs_0_.basis_ref, f32[2,2,16]{2,1,0:T(2,128)S(1)} %get-tuple-element.31.refs_1_.coef_ref.refs_2_.refs_4_, ...), custom_call_target="tpu_custom_call" | custom-call | flops 1000000 | bytes 1000000 | tf_op jit(solution)/shard_map/pallas_call | solution.py:766
  12.4 0.0 collective-permute-start.4
  12.5 2.6 %collective-permute-start.5 = (f32[8,256]{1,0:T(8,128)S(1)}, f32[8,256]{1,0:T(8,128)S(1)}, u32[]{:S(2)}, u32[]{:S(2)}) collective-permute-start(f32[8,256]{1,0:T(8,128)S(1)} %get-tuple-element.47), channel_id=1, source_target_pairs={{4,0},{8,4},{12,8},{16,12},{20,16},{24,20},{28,24},{0,28},{5,1},{9... | collective-permute-start | bytes 24584 | tf_op jit(solution)/shard_map/ppermute | solution.py:785
  15.1 1.3 %collective-permute-start.6 = (f32[8,256]{1,0:T(8,128)S(1)}, f32[8,256]{1,0:T(8,128)S(1)}, u32[]{:S(2)}, u32[]{:S(2)}) collective-permute-start(f32[8,256]{1,0:T(8,128)S(1)} %get-tuple-element.48), channel_id=1, source_target_pairs={{0,1},{1,2},{2,3},{3,0},{4,5},{5,6},{6,7},{7,4},{8,9},{9,10},{10,1... | collective-permute-start | bytes 24584 | tf_op jit(solution)/shard_map/ppermute | solution.py:785
  16.4 2.5 %collective-permute-start.7 = (f32[8,256]{1,0:T(8,128)S(1)}, f32[8,256]{1,0:T(8,128)S(1)}, u32[]{:S(2)}, u32[]{:S(2)}) collective-permute-start(f32[8,256]{1,0:T(8,128)S(1)} %get-tuple-element.49), channel_id=1, source_target_pairs={{1,0},{2,1},{3,2},{0,3},{5,4},{6,5},{7,6},{4,7},{9,8},{10,9},{11,1... | collective-permute-start | bytes 24584 | tf_op jit(solution)/shard_map/ppermute | solution.py:785
  18.9 2.4 %shard_map.97 = (f32[8,384]{1,0:T(8,128)S(1)}, f32[16,2,2,16,512]{4,3,2,1,0:T(8,128)S(1)}, f32[2,2,16,512]{3,2,1,0:T(8,128)S(1)}) custom-call(f32[4,2,2,16,512]{4,3,2,1,0:T(8,128)S(1)} %get-tuple-element.30.refs_0_.basis_ref, f32[2,2,16]{2,1,0:T(2,128)S(1)} %get-tuple-element.31.refs_1_.coef_ref.refs_2_.refs_4_, ...), custom_call_target="tpu_custom_call" | custom-call | flops 1000000 | bytes 1000000 | tf_op jit(solution)/shard_map/pallas_call | solution.py:766
  21.3 0.0 collective-permute-done.4.refs_8_
  21.3 0.0 collective-permute-done.5.refs_9_
  21.3 0.0 collective-permute-done.6.refs_10_
  21.3 0.0 collective-permute-done.7.refs_11_
  21.3 0.8 %shard_map.98 = (f32[2,2,16,512]{3,2,1,0:T(8,128)S(1)}, f32[256,128]{1,0:T(8,128)S(1)}) custom-call(f32[4,2,2,16,512]{4,3,2,1,0:T(8,128)S(1)} %get-tuple-element.30.refs_0_.basis_ref, f32[2,2,16,512]{3,2,1,0:T(8,128)S(1)} %get-tuple-element.41.refs_1_, f32[2,2,16]{2,1,0:T(2,128)S(1)} %get-tuple-element.31.refs_1_.coef_ref.refs_2_.refs_4_, ...), custom_call_target="tpu_custom_call" | custom-call | flops 1000000 | bytes 1000000 | tf_op jit(solution)/shard_map/pallas_call | solution.py:766
  22.2 12.7 %all_to_all.11 = f32[32,8,128]{2,1,0:T(8,128)S(1)} all-to-all(f32[32,8,128]{2,1,0:T(8,128)S(1)} %bitcast.3), channel_id=1, replica_groups=mesh['bx'=8,'by'=4] {'bx','by'}, dimensions={0} | all-to-all | bytes 262144 | tf_op jit(solution)/shard_map/all_to_all | solution.py:840
  34.9 2.1 %shard_map.99 = (f32[2,2,16,512]{3,2,1,0:T(8,128)}, f32[2,2,16,512]{3,2,1,0:T(8,128)}, f32[5]{0:T(128)}) custom-call(f32[4,2,2,16,512]{4,3,2,1,0:T(8,128)S(1)} %get-tuple-element.30.refs_0_.basis_ref, f32[2,2,16,512]{3,2,1,0:T(8,128)S(1)} %get-tuple-element.41.refs_1_, f32[2,2,16,512]{3,2,1,0:T(8,128)S(1)} %get-tuple-element.54.refs_2_, ...), custom_call_target="tpu_custom_call" | custom-call | flops 1000000 | bytes 1000000 | tf_op jit(solution)/shard_map/pallas_call | solution.py:766
Async XLA Ops:
  2.0 9.7 %collective-permute-start = (f32[16,256]{1,0:T(8,128)S(1)}, f32[16,256]{1,0:T(8,128)S(1)}, u32[]{:S(2)}, u32[]{:S(2)}) collective-permute-start(f32[16,256]{1,0:T(8,128)S(1)} %get-tuple-element.37), channel_id=1, source_target_pairs={{0,4},{4,8},{8,12},{12,16},{16,20},{20,24},{24,28},{28,0},{1,5},{5... | collective-permute-start | bytes 49160 | tf_op jit(solution)/shard_map/ppermute | solution.py:785
  2.5 9.1 %collective-permute-start.1 = (f32[16,256]{1,0:T(8,128)S(1)}, f32[16,256]{1,0:T(8,128)S(1)}, u32[]{:S(2)}, u32[]{:S(2)}) collective-permute-start(f32[16,256]{1,0:T(8,128)S(1)} %get-tuple-element.38), channel_id=1, source_target_pairs={{4,0},{8,4},{12,8},{16,12},{20,16},{24,20},{28,24},{0,28},{5,1},{9... | collective-permute-start | bytes 49160 | tf_op jit(solution)/shard_map/ppermute | solution.py:785
  5.4 6.2 %collective-permute-start.2 = (f32[16,256]{1,0:T(8,128)S(1)}, f32[16,256]{1,0:T(8,128)S(1)}, u32[]{:S(2)}, u32[]{:S(2)}) collective-permute-start(f32[16,256]{1,0:T(8,128)S(1)} %get-tuple-element.39), channel_id=1, source_target_pairs={{0,1},{1,2},{2,3},{3,0},{4,5},{5,6},{6,7},{7,4},{8,9},{9,10},{10,1... | collective-permute-start | bytes 49160 | tf_op jit(solution)/shard_map/ppermute | solution.py:785
  7.7 4.0 %collective-permute-start.3 = (f32[16,256]{1,0:T(8,128)S(1)}, f32[16,256]{1,0:T(8,128)S(1)}, u32[]{:S(2)}, u32[]{:S(2)}) collective-permute-start(f32[16,256]{1,0:T(8,128)S(1)} %get-tuple-element.40), channel_id=1, source_target_pairs={{1,0},{2,1},{3,2},{0,3},{5,4},{6,5},{7,6},{4,7},{9,8},{10,9},{11,1... | collective-permute-start | bytes 49160 | tf_op jit(solution)/shard_map/ppermute | solution.py:785
  12.4 8.9 %collective-permute-start.4 = (f32[8,256]{1,0:T(8,128)S(1)}, f32[8,256]{1,0:T(8,128)S(1)}, u32[]{:S(2)}, u32[]{:S(2)}) collective-permute-start(f32[8,256]{1,0:T(8,128)S(1)} %get-tuple-element.46), channel_id=1, source_target_pairs={{0,4},{4,8},{8,12},{12,16},{16,20},{20,24},{24,28},{28,0},{1,5},{5... | collective-permute-start | bytes 24584 | tf_op jit(solution)/shard_map/ppermute | solution.py:785
  12.5 8.8 %collective-permute-start.5 = (f32[8,256]{1,0:T(8,128)S(1)}, f32[8,256]{1,0:T(8,128)S(1)}, u32[]{:S(2)}, u32[]{:S(2)}) collective-permute-start(f32[8,256]{1,0:T(8,128)S(1)} %get-tuple-element.47), channel_id=1, source_target_pairs={{4,0},{8,4},{12,8},{16,12},{20,16},{24,20},{28,24},{0,28},{5,1},{9... | collective-permute-start | bytes 24584 | tf_op jit(solution)/shard_map/ppermute | solution.py:785
  15.1 6.2 %collective-permute-start.6 = (f32[8,256]{1,0:T(8,128)S(1)}, f32[8,256]{1,0:T(8,128)S(1)}, u32[]{:S(2)}, u32[]{:S(2)}) collective-permute-start(f32[8,256]{1,0:T(8,128)S(1)} %get-tuple-element.48), channel_id=1, source_target_pairs={{0,1},{1,2},{2,3},{3,0},{4,5},{5,6},{6,7},{7,4},{8,9},{9,10},{10,1... | collective-permute-start | bytes 24584 | tf_op jit(solution)/shard_map/ppermute | solution.py:785
  16.4 4.9 %collective-permute-start.7 = (f32[8,256]{1,0:T(8,128)S(1)}, f32[8,256]{1,0:T(8,128)S(1)}, u32[]{:S(2)}, u32[]{:S(2)}) collective-permute-start(f32[8,256]{1,0:T(8,128)S(1)} %get-tuple-element.49), channel_id=1, source_target_pairs={{1,0},{2,1},{3,2},{0,3},{5,4},{6,5},{7,6},{4,7},{9,8},{10,9},{11,1... | collective-permute-start | bytes 24584 | tf_op jit(solution)/shard_map/ppermute | solution.py:785
where the time goes:
time: 37.2 us; the launch traced here: 37.1 us
  starting transfers between devices  14.3 us (38%)
  blocking collectives  12.7 us (34%)
  Pallas kernels  9.31 us (25%)
  between operations  0.71 us (2%)
    ppermute x8, starting transfers between devices, exchange(): out[place] = lax.ppermute(sends[place], axis, ring)  14.3 us
    all_to_all x1, blocking collectives, one_exchange(): got = lax.all_to_all(row, ('bx', 'by'), 0, 0, tiled=True)  12.7 us
    pallas_call x6, Pallas kernels, call(): pl.pallas_call(kernel, out_shape=[jax.ShapeDtypeStruct(shape, dtype) for...  9.31 us
  transfers between devices with their start and end apart: 8, of which 0 were waited for; matrix products, arithmetic and copies ran while one was open for 0% of the time, Pallas kernels for 12%

commit v1 on v0

--- a/solution.py
+++ b/solution.py
@@ -20,6 +20,8 @@
 VMEM_BYTES = 12 << 20
 HALF = 8
 XY = 4 * EX * EY
+AT_G, AT_FAR, AT_R, AT_SUM, AT_GRAM, AT_ID = 64, 80, 88, 96, 112, 122
+SENT = 2
 VERTS = 4 * CGZ
 
 PENALTY = 2.0
@@ -121,15 +123,23 @@
 
 
 def pack_all(groups):
-    return [
-        pack_x([groups[EX - 1][y] for y in range(EY)], True),
-        pack_x([groups[0][y] for y in range(EY)], False),
-        pack_y([groups[x][EY - 1] for x in range(EX)], True),
-        pack_y([groups[x][0] for x in range(EX)], False),
-    ]
+    right = pack_x([groups[EX - 1][y] for y in range(EY)], True)
+    left = pack_x([groups[0][y] for y in range(EY)], False)
+    back = pack_y([groups[x][EY - 1] for x in range(EX)], True)
+    front = pack_y([groups[x][0] for x in range(EX)], False)
+    return [*pair_up(right, left, "bx"), *pair_up(back, front, "by")]
+
+
+def pair_up(first, second, axis):
+    place = jnp.full(first.shape, lax.rem(lax.axis_index(axis), 2), jnp.int32)
+    even = place == 0
+    return jnp.where(even, first, second), jnp.where(even, second, first)
 
 
 def unpack_all(packed):
+    right, left = pair_up(packed[0], packed[1], "bx")
+    back, front = pair_up(packed[2], packed[3], "by")
+    packed = (left, right, front, back)
     left = unpack_x(packed[0], False)
     right = unpack_x(packed[1], True)
     front = unpack_y(packed[2], False)
@@ -298,11 +308,9 @@
         copy.wait()
     lane = lane_ids(1, LANES)
     row = jnp.zeros((1, LANES), F32)
-    for a in range(2):
-        for b in range(2):
-            short = ids_scratch[0, 0, a, b : b + 1, :].astype(F32)
-            for level in range(CGZ):
-                row = jnp.where(lane == 80 + (a * 2 + b) * CGZ + level, short[:, level : level + 1], row)
+    short = ids_scratch[0, 0, 0, 0:1, :].astype(F32)
+    for level in range(CGZ):
+        row = jnp.where(lane == AT_ID + level, short[:, level : level + 1], row)
     ids_ref[...] = jnp.broadcast_to(row, (8, LANES))
 
 
@@ -311,10 +319,10 @@
     return jnp.dot(matrix, pick, precision=HIGHEST, preferred_element_type=F32)
 
 
-def tables_kernel(modes_ref, eigen_ref, sb_ref, st_ref, lh_ref, ll_ref, xy_ref, z_ref):
+def tables_kernel(modes_ref, eigen_ref, sb_ref, lh_ref, ll_ref, lx_ref, xy_ref, z_ref):
     strides = (PTS * PTS, PTS, 1)
     eye = (row_ids(PTS, PTS) == lane_ids(PTS, PTS)).astype(F32)
-    straight, turned, stiff, unit = [], [], [], []
+    straight, stiff, unit = [], [], []
     for d in range(3):
         mode = modes_ref[d]
         turn = lax.dot_general(
@@ -323,7 +331,6 @@
         scaled = mode * eigen_ref[d : d + 1, :]
         one = jnp.dot(scaled, turn, precision=HIGHEST, preferred_element_type=F32)
         straight.append(expand(mode, strides[d]))
-        turned.append(expand(turn, strides[d]))
         stiff.append(expand(one, strides[d]))
         unit.append(expand(eye, strides[d]))
     for i in range(PTS):
@@ -331,14 +338,21 @@
             rows = slice((i * PTS + j) * PTS, (i * PTS + j + 1) * PTS)
             pair = straight[0][i : i + 1] * straight[1][j : j + 1]
             sb_ref[rows, :] = (pair * straight[2]).astype(BF16)
-            pair = turned[0][i : i + 1] * turned[1][j : j + 1]
-            st_ref[rows, :] = (pair * turned[2]).astype(BF16)
-            both = unit[0][i : i + 1] * unit[1][j : j + 1]
-            either = stiff[0][i : i + 1] * unit[1][j : j + 1] + unit[0][i : i + 1] * stiff[1][j : j + 1]
-            full = either * unit[2] + both * stiff[2]
+    lane = lane_ids(8, LANES)
+    for half in range(2):
+        for j in range(PTS):
+            rows = slice((half * PTS + j) * PTS, (half * PTS + j + 1) * PTS)
+            full = stiff[1][j : j + 1, :LANES] * unit[2][:, :LANES]
+            full = full + unit[1][j : j + 1, :LANES] * stiff[2][:, :LANES]
+            full = jnp.where(lane // 64 == half, full, 0.0)
             head = full.astype(BF16)
             lh_ref[rows, :] = head
             ll_ref[rows, :] = (full - head.astype(F32)).astype(BF16)
+    low_half = lane_ids(1, NODES) % LANES < 64
+    for c in range(NODES // LANES):
+        even, odd = stiff[0][2 * c : 2 * c + 1], stiff[0][2 * c + 1 : 2 * c + 2]
+        lx_ref[c : c + 1, :] = jnp.where(low_half, even, odd)
+        lx_ref[c + 4 : c + 5, :] = jnp.where(low_half, odd, even)
     point, row = lane_ids(PTS, PTS), row_ids(PTS, PTS)
     pairs = (row < 2 * EX, row // 2 * (PTS - 1) + point, row % 2)
     short = jnp.maximum(
@@ -379,9 +393,9 @@
 
 
 def smooth_kernel(*refs):
-    basis_ref, coef_ref, mask_ref, eigen_ref, sb_ref, st_ref = refs[:6]
-    halo = [ref[0:8, :] for ref in refs[6:10]]
-    smooth_ref, *send = refs[10:]
+    basis_ref, coef_ref, mask_ref, eigen_ref, sb_ref = refs[:5]
+    halo = [ref[0:8, :] for ref in refs[5:9]]
+    smooth_ref, *send = refs[9:]
     current = load_groups(basis_ref, KV - 1)
     inside, outside = own_neighbors(current), unpack_all(halo)
     coef, active = columns(coef_ref), columns(mask_ref)
@@ -394,7 +408,12 @@
     modal = [
         [modal[x][y] / (coef[x][y] * spectrum + SHIFT) for y in range(EY)] for x in range(EX)
     ]
-    smooth = jnp.dot(stack(modal).astype(BF16), st_ref[...], preferred_element_type=F32)
+    smooth = lax.dot_general(
+        stack(modal).astype(BF16),
+        sb_ref[...],
+        (((1,), (1,)), ((), ())),
+        preferred_element_type=F32,
+    )
     smooth = unstack(smooth)
     smooth = [[smooth[x][y] * active[x][y] for y in range(EY)] for x in range(EX)]
     for x in range(EX):
@@ -404,20 +423,31 @@
         ref[...] = face
 
 
-def stiff_apply(groups, lh_ref, ll_ref):
+def stiff_apply(groups, lh_ref, ll_ref, lx_ref):
     whole = stack(groups)
-    head = whole.astype(BF16)
-    tail = (whole - head.astype(F32)).astype(BF16)
-    rows = whole.shape[0]
+    chunks = [whole[:, c : c + LANES] for c in range(0, NODES, LANES)]
+    tall = jnp.concatenate(chunks, axis=0)
+    head = tall.astype(BF16)
+    tail = (tall - head.astype(F32)).astype(BF16)
+    rows, size = tall.shape[0], whole.shape[0]
     both = jnp.dot(jnp.concatenate([head, tail], axis=0), lh_ref[...], preferred_element_type=F32)
-    low = jnp.dot(head, ll_ref[...], preferred_element_type=F32)
-    return unstack(both[:rows] + (both[rows:] + low))
+    inner = both[:rows] + (both[rows:] + jnp.dot(head, ll_ref[...], preferred_element_type=F32))
+    turned = [pltpu.roll(chunk, 64, 1) for chunk in chunks]
+    out = []
+    for c in range(len(chunks)):
+        lanes = slice(c * LANES, (c + 1) * LANES)
+        total = inner[c * size : (c + 1) * size]
+        for d in range(len(chunks)):
+            total = total + chunks[d] * lx_ref[d : d + 1, lanes]
+            total = total + turned[d] * lx_ref[d + 4 : d + 5, lanes]
+        out.append(total)
+    return unstack(jnp.concatenate(out, axis=1))
 
 
 def image_kernel(count, *refs):
-    basis_ref, smooth_ref, coef_ref, mask_ref, ids_ref, got_ref, lh_ref, ll_ref = refs[:8]
-    face_refs, mask_refs = refs[8:12], refs[12:16]
-    precond_ref, image_ref, row_ref = refs[16:]
+    basis_ref, smooth_ref, coef_ref, mask_ref, ids_ref, got_ref, lh_ref, ll_ref, lx_ref = refs[:9]
+    face_refs, mask_refs = refs[9:13], refs[13:17]
+    precond_ref, image_ref, row_ref = refs[17:]
     coef, active = columns(coef_ref), columns(mask_ref)
     solved = got_ref[...]
     lane = lane_ids(1, count)
@@ -436,7 +466,7 @@
     precond = [
         [smooth[x][y] + active[x][y] * field[x][y] for y in range(EY)] for x in range(EX)
     ]
-    stiff = stiff_apply(precond, lh_ref, ll_ref)
+    stiff = stiff_apply(precond, lh_ref, ll_ref, lx_ref)
     inside = own_neighbors(precond)
     outside = unpack_all([ref[...] for ref in face_refs])
     open_faces = unpack_all([ref[8:16, :] for ref in mask_refs])
@@ -594,12 +624,19 @@
     for v in range(KV):
         for u in range(v, KV):
             position[v, u] = len(position)
-    products(vectors, lambda half: None, halves, lambda v, u, s: put(96 + position[v, u], s))
+
+    def put_field(v, w, value):
+        far = (w - v) % VERTS
+        if far > VERTS // 2 or (far == VERTS // 2 and v > w):
+            v, far = w, VERTS - far
+        put(LANES + AT_FAR + v if far == VERTS // 2 else far * VERTS + v, value)
+
+    products(vectors, lambda half: None, halves, lambda v, u, s: put(LANES + AT_GRAM + position[v, u], s))
     for ab in range(4):
-        products(vectors, fields(ab), halves, lambda v, w, s: put(v * VERTS + w, s))
-        products(fields(ab), lambda half: None, halves, lambda v, w, s: put(LANES + v * VERTS + w, s))
+        products(vectors, fields(ab), halves, lambda v, w, s: put(LANES + v * VERTS + w, s))
+        products(fields(ab), lambda half: None, halves, put_field)
         for other in range(ab + 1, 4):
-            products(fields(ab), fields(other), halves, lambda v, w, s: put(LANES + v * VERTS + w, s))
+            products(fields(ab), fields(other), halves, put_field)
     for level in range(CGZ):
         sums = [[None] * EY for _ in range(EX)]
         for x in range(EX):
@@ -612,17 +649,18 @@
                     at = (ab * EX + x) * EY + y
                     total = total + sums[x][y] * xy_ref[at : at + 1, :]
             parts = [total[:, c : c + LANES] for c in range(0, NODES, LANES)]
-            put(64 + ab * CGZ + level, functools.reduce(jnp.add, parts) * scale)
+            put(LANES + AT_SUM + ab * CGZ + level, functools.reduce(jnp.add, parts) * scale)
     early_ref[...] = lane_sums(rows_ref[...])
 
 
 def base_kernel(rows, peers, *refs):
-    basis_ref, smooth_ref, coef_ref, mask_ref, ids_ref, inverse_ref, lh_ref, ll_ref = refs[:8]
-    face_refs, early_ref, field_ref = refs[8:12], refs[12], refs[13]
-    base_ref, send_ref, rows_ref = refs[14:]
+    basis_ref, smooth_ref, coef_ref, mask_ref, ids_ref, inverse_ref = refs[:6]
+    lh_ref, ll_ref, lx_ref = refs[6:9]
+    face_refs, early_ref, field_ref = refs[9:13], refs[13], refs[14]
+    base_ref, send_ref, rows_ref = refs[15:]
     coef, active = columns(coef_ref), columns(mask_ref)
     smooth = load_groups(smooth_ref)
-    stiff = stiff_apply(smooth, lh_ref, ll_ref)
+    stiff = stiff_apply(smooth, lh_ref, ll_ref, lx_ref)
     inside = own_neighbors(smooth)
     outside = unpack_all([ref[...] for ref in face_refs])
     counts = face_count(EZ)
@@ -656,106 +694,144 @@
     def put(row, value):
         rows_ref[row : row + 1, :] = value
 
-    products(base, vectors, halves, lambda v, w, s: put(w, s))
+    products(base, vectors, halves, lambda v, w, s: put(AT_R + w, s))
     for part in range(VERTS // 8):
-        products(base, fields(part), halves, lambda v, w, s: put(VERTS + w, s))
+        products(base, fields(part), halves, lambda v, w, s: put(AT_G + w, s))
     late = lane_sums(rows_ref[...])
-    lane, row = lane_ids(8, LANES), row_ids(8, LANES)
     early = early_ref[...]
-    tile = early[:, :LANES]
-    tile = jnp.where(jnp.logical_and(lane >= 80, lane < 80 + VERTS), ids_ref[...], tile)
-    tile = jnp.where(row == 1, early[:, LANES : 2 * LANES], tile)
-    tile = jnp.where(row == 2, early[:, 2 * LANES :], tile)
-    tile = jnp.where(row == 3, late, tile)
     first = lax.axis_index("by") * rows
-    for r in range(rows):
-        tile = jnp.where(row == 4 + r, inverse_ref[pl.ds(first + r, 1), :], tile)
+    tile = jnp.concatenate(
+        [early[0:1, :LANES], early[0:1, LANES:] + late[0:1] + ids_ref[0:1, :]]
+        + [inverse_ref[pl.ds(first + r, 1), :] for r in range(rows)],
+        axis=0,
+    )
+    size = SENT + rows
     for peer in range(peers):
-        send_ref[8 * peer : 8 * peer + 8, :] = tile
+        send_ref[size * peer : size * peer + size, :] = tile
 
 
 def close_kernel(total_points, rows, peers, *refs):
-    basis_ref, smooth_ref, base_ref, wall_ref, coef_ref, mask_ref, ids_ref = refs[:7]
-    xy_ref, z_ref, got_ref, precond_ref, next_ref, hessen_ref = refs[7:]
+    basis_ref, smooth_ref, base_ref, wall_ref, coef_ref, mask_ref = refs[:6]
+    xy_ref, z_ref, got_ref, precond_hbm, next_hbm, hessen_ref = refs[6:12]
+    precond_ref, next_ref, sems = refs[12:]
     lane, row = lane_ids(peers, LANES), row_ids(peers, LANES)
+    side = lax.axis_size("by")
 
     def got(r):
-        return got_ref[pl.ds(r, peers, stride=8), :]
-
-    sums, late = got(0), got(3)
+        return got_ref[pl.ds(r, peers, stride=SENT + rows), :]
+
+    def along_x(values, step):
+        return pltpu.roll(values, (step * side) % peers, 0)
+
+    def along_y(values, step):
+        edge = row % side == (0 if step > 0 else side - 1)
+        wrapped = pltpu.roll(values, (step * (1 - side)) % peers, 0)
+        return jnp.where(edge, wrapped, pltpu.roll(values, step % peers, 0))
+
+    def turn(values, lanes):
+        return pltpu.roll(values, (-lanes) % LANES, 1)
+
+    sums = got(1)
+    corner = sums + along_x(turn(sums, 2 * CGZ), 1)
+    other = turn(sums, CGZ) + along_x(turn(sums, 3 * CGZ), 1)
+    corner = corner + along_y(other, 1)
     number = lane.astype(F32)
-    hits = [number == sums[:, 80 + v : 81 + v] for v in range(VERTS)]
+    hits = [number == sums[:, AT_ID + v : AT_ID + v + 1] for v in range(CGZ)]
     coarse = jnp.zeros((peers, LANES), F32)
-    for v in range(VERTS):
-        coarse = coarse + jnp.where(hits[v], sums[:, 64 + v : 65 + v], 0.0)
+    for v in range(CGZ):
+        coarse = coarse + jnp.where(hits[v], corner[:, AT_SUM + v : AT_SUM + v + 1], 0.0)
     coarse = fold(coarse)
     solved = jnp.zeros((peers, LANES), F32)
     for r in range(rows):
         part = jnp.where(lane == row * rows + r, coarse, 0.0)
-        solved = solved + jnp.sum(part, axis=1, keepdims=True) * got(4 + r)
+        solved = solved + jnp.sum(part, axis=1, keepdims=True) * got(SENT + r)
     solved = fold(solved)
-    spread = jnp.zeros((peers, LANES), F32)
-    wide = [jnp.zeros((peers, LANES), F32) for _ in range(2)]
-    for v in range(VERTS):
+    near = jnp.zeros((peers, LANES), F32)
+    for v in range(CGZ):
         value = jnp.sum(jnp.where(hits[v], solved, 0.0), axis=1, keepdims=True)
-        spread = jnp.where(lane % VERTS == v, value, spread)
-        part = v * VERTS // LANES
-        wide[part] = jnp.where(lane // VERTS == v - part * 8, value, wide[part])
-    upper = [lane % VERTS > lane // VERTS + part * 8 for part in range(2)]
-    twice = [jnp.where(u, 2.0, 1.0) for u in upper]
-    quad = (got(1) * wide[0] * twice[0] + got(2) * wide[1] * twice[1]) * spread
-    linear = fold(sums * spread)
-    late_sum = fold(late)
-    in_g = jnp.logical_and(lane >= VERTS, lane < 2 * VERTS)
-    square = quad + jnp.where(in_g, 2.0 * late * spread, 0.0) + jnp.where(lane == KV, late, 0.0)
+        near = jnp.where(lane % CGZ == v, value, near)
+    right = along_x(near, -1)
+    quarter = lane % VERTS // CGZ
+    lower = jnp.where(quarter < 2, near, right)
+    spread = jnp.where(quarter % 2 == 0, lower, along_y(lower, -1))
+    me = lax.axis_index("bx") * side + lax.axis_index("by")
+    own = fold(jnp.where(row == me, spread, 0.0))
+    coef, active = columns(coef_ref), columns(mask_ref)
+    along, bent = [], []
+    for ab in range(4):
+        plain = jnp.zeros((EZ, NODES), F32)
+        stiff = jnp.zeros((EZ, NODES), F32)
+        for level in range(CGZ):
+            value = own[:, ab * CGZ + level : ab * CGZ + level + 1]
+            plain = plain + value * z_ref[level * EZ : (level + 1) * EZ, :]
+            stiff = stiff + value * z_ref[(CGZ + level) * EZ : (CGZ + level + 1) * EZ, :]
+        along.append(plain)
+        bent.append(stiff)
+    copies, fields = [], []
+    for x in range(EX):
+        for y in range(EY):
+            field = jnp.zeros((EZ, NODES), F32)
+            for ab in range(4):
+                at = (ab * EX + x) * EY + y
+                field = field + along[ab] * xy_ref[at : at + 1, :]
+            precond_ref[x, y] = smooth_ref[x, y] + active[x][y] * field
+            n = len(copies)
+            copies.append(
+                pltpu.make_async_copy(precond_ref.at[x, y], precond_hbm.at[x, y], sems.at[n])
+            )
+            copies[-1].start()
+            fields.append(field)
+    group = lane // VERTS
+    shifted = spread
+    for far in range(1, VERTS // 2):
+        shifted = jnp.where(group == far, turn(spread, far), shifted)
+    weight = jnp.where(group == 0, 1.0, 2.0)
+    square = got(0) * spread * shifted * weight
+    scaled = sums * spread
+    square = square + jnp.where(group == AT_G // VERTS, 2.0 * scaled, 0.0)
+    distant = jnp.logical_and(lane >= AT_FAR, lane < AT_FAR + VERTS // 2)
+    square = square + jnp.where(distant, 2.0 * scaled * turn(spread, VERTS // 2), 0.0)
+    square = square + jnp.where(lane == AT_R + KV, sums, 0.0)
     square = jnp.sum(fold(square), axis=1, keepdims=True) / total_points
+    linear, plain = fold(scaled), fold(sums)
     line = lane_ids(1, LANES)
     proj = []
     for v in range(KV):
-        term = jnp.where(line // VERTS == v, linear, 0.0) + jnp.where(line == v, late_sum, 0.0)
+        term = jnp.where(line // VERTS == v, linear, 0.0) + jnp.where(line == AT_R + v, plain, 0.0)
         proj.append(jnp.sum(term, axis=1, keepdims=True) / total_points)
     pair = jnp.zeros((1, LANES), F32)
-    position = 96
+    position = AT_GRAM
     for v in range(KV):
         for u in range(v, KV):
             factor = 1.0 if u == v else 2.0
             pair = jnp.where(line == position, factor * proj[v] * proj[u], pair)
             position += 1
-    gram = jnp.sum(pair * fold(sums), axis=1, keepdims=True) / total_points
+    gram = jnp.sum(pair * plain, axis=1, keepdims=True) / total_points
     dot = functools.reduce(jnp.add, [p * p for p in proj])
     beta = jnp.sqrt(square - 2.0 * dot + gram + EPSILON)
-    coef, active = columns(coef_ref), columns(mask_ref)
-    along, bent = [], []
-    for a in range(2):
-        for b in range(2):
-            plain = jnp.zeros((EZ, NODES), F32)
-            stiff = jnp.zeros((EZ, NODES), F32)
-            for level in range(CGZ):
-                at = 80 + (a * 2 + b) * CGZ + level
-                hit = jnp.where(line.astype(F32) == ids_ref[0:1, at : at + 1], solved, 0.0)
-                value = jnp.sum(hit, axis=1, keepdims=True)
-                plain = plain + value * z_ref[level * EZ : (level + 1) * EZ, :]
-                stiff = stiff + value * z_ref[(CGZ + level) * EZ : (CGZ + level + 1) * EZ, :]
-            along.append(plain)
-            bent.append(stiff)
+    inverse = 1.0 / beta
     for x in range(EX):
         for y in range(EY):
-            field = jnp.zeros((EZ, NODES), F32)
             image = jnp.zeros((EZ, NODES), F32)
             for ab in range(4):
                 at = (ab * EX + x) * EY + y
-                plain = xy_ref[at : at + 1, :]
-                field = field + along[ab] * plain
-                image = image + (along[ab] * xy_ref[XY + at : XY + at + 1, :] + bent[ab] * plain)
-            precond_ref[x, y] = smooth_ref[x, y] + active[x][y] * field
-            residual = (
-                base_ref[x, y] + (active[x][y] * coef[x][y]) * image + wall_ref[x, y] * field
-            )
+                image = image + (
+                    along[ab] * xy_ref[XY + at : XY + at + 1, :] + bent[ab] * xy_ref[at : at + 1, :]
+                )
+            residual = base_ref[x, y] + (active[x][y] * coef[x][y]) * image
+            residual = residual + wall_ref[x, y] * fields[x * EY + y]
             for v in range(KV):
                 residual = residual - proj[v] * basis_ref[v, x, y]
-            next_ref[x, y] = residual / beta
+            next_ref[x, y] = residual * inverse
+            n = len(copies)
+            copies.append(pltpu.make_async_copy(next_ref.at[x, y], next_hbm.at[x, y], sems.at[n]))
+            copies[-1].start()
+    result = jnp.zeros((1, LANES), F32)
     for v, value in enumerate(proj + [beta]):
-        hessen_ref[v] = jnp.sum(value)
+        result = jnp.where(line == v, value, result)
+    hessen_ref[...] = result[:, : KV + 1]
+    for copy in copies:
+        copy.wait()
 
 
 def spec(kind=pltpu.VMEM):
@@ -776,13 +852,13 @@
 
 def exchange(sends):
     out = [None] * 4
-    for place in (3, 2, 1, 0):
+    for place in range(4):
         axis = "bx" if place < 2 else "by"
         size = lax.axis_size(axis)
-        ring = [(i, (i + 1) % size) for i in range(size)]
-        if place % 2:
-            ring = [(j, i) for i, j in ring]
-        out[place] = lax.ppermute(sends[place], axis, ring)
+        assert size % 2 == 0
+        pairs = [(i, (i + 1) % size) for i in range(place % 2, size, 2)]
+        pairs = pairs + [(j, i) for i, j in pairs]
+        out[place] = lax.ppermute(sends[place], axis, pairs)
     return out
 
 
@@ -791,15 +867,17 @@
     square = ((NODES, NODES), BF16)
     tables = call(
         tables_kernel,
-        [square] * 4 + [((2 * XY, NODES), F32), ((2 * CGZ * EZ, NODES), F32)],
+        [square]
+        + [((LANES, LANES), BF16)] * 2
+        + [((8, NODES), F32), ((2 * XY, NODES), F32), ((2 * CGZ * EZ, NODES), F32)],
         [spec()] * 2,
         (modes, eigen),
     )
     smooth, *sends = call(
         smooth_kernel,
         [FIELD] + [((8, 256), F32)] * 4,
-        [spec()] * 10,
-        (basis, coef, mask, eigen, tables[0], tables[1], *halo),
+        [spec()] * 9,
+        (basis, coef, mask, eigen, tables[0], *halo),
     )
     return halo, tables, smooth, exchange(sends)
 
@@ -825,26 +903,29 @@
     halo, tables, smooth, faces = smooth_part(basis, coef, modes, eigen, mask, (a, b, c, d))
     early, fields, wall = call(
         functools.partial(fields_kernel, 1.0 / math.sqrt(points)),
-        [((8, 3 * LANES), F32), ((VERTS,) + FIELD[0], F32), FIELD],
+        [((8, 2 * LANES), F32), ((VERTS,) + FIELD[0], F32), FIELD],
         [spec()] * 9,
         (basis, coef, mask, *halo, tables[4], tables[5]),
-        scratch=[pltpu.VMEM((3 * LANES, LANES), F32)],
+        scratch=[pltpu.VMEM((2 * LANES, LANES), F32)],
     )
     base, row = call(
         functools.partial(base_kernel, rows, peers),
-        [FIELD, ((8 * peers, LANES), F32)],
-        [spec()] * 14,
-        (basis, smooth, coef, mask, ids, coarse_inverse, *tables[2:4], *faces, early, fields),
+        [FIELD, (((SENT + rows) * peers, LANES), F32)],
+        [spec()] * 15,
+        (basis, smooth, coef, mask, ids, coarse_inverse, *tables[1:4], *faces, early, fields),
         scratch=[pltpu.VMEM((LANES, LANES), F32)],
     )
-    got = lax.all_to_all(row, ("bx", "by"), 0, 0, tiled=True)
-    return call(
+    row = row.reshape(peers, SENT + rows, 1, LANES)
+    got = lax.all_to_all(row, ("bx", "by"), 0, 0).reshape((SENT + rows) * peers, LANES)
+    precond, next_vector, hessen = call(
         functools.partial(close_kernel, float(points * peers), rows, peers),
-        [FIELD, FIELD, ((KV + 1,), F32)],
-        [spec()] * 10,
-        (basis, smooth, base, wall, coef, mask, ids, tables[4], tables[5], got),
-        out_specs=[spec(), spec(), spec(pltpu.SMEM)],
-    )
+        [FIELD, FIELD, ((1, KV + 1), F32)],
+        [spec()] * 9,
+        (basis, smooth, base, wall, coef, mask, tables[4], tables[5], got),
+        out_specs=[spec(pltpu.HBM), spec(pltpu.HBM), spec()],
+        scratch=[pltpu.VMEM(*FIELD), pltpu.VMEM(*FIELD), pltpu.SemaphoreType.DMA((2 * EX * EY,))],
+    )
+    return precond, next_vector, hessen.reshape(KV + 1)
 
 
 def two_exchanges(basis, coef, modes, eigen, mask, vertex_ids, coarse_inverse):
@@ -864,8 +945,8 @@
     precond, image, row = call(
         functools.partial(image_kernel, count),
         [FIELD, FIELD, ((1, LANES), F32)],
-        [spec()] * 4 + [spec(pltpu.SMEM)] + [spec()] * 11,
-        (basis, smooth, coef, mask, vertex_ids, solved, tables[2], tables[3], *faces, *halo),
+        [spec()] * 4 + [spec(pltpu.SMEM)] + [spec()] * 12,
+        (basis, smooth, coef, mask, vertex_ids, solved, *tables[1:4], *faces, *halo),
     )
     row = lax.psum(row, ("bx", "by"))
     next_vector, hessen = call(

time: 37.2 us -> 34.6 us (0.930)
  starting transfers between devices: 14.3 us -> 11.3 us
  waiting for transfers between devices: 0.04 us -> 2.53 us
  blocking collectives: 12.7 us -> 11.5 us
  Pallas kernels: 9.31 us -> 8.41 us
    ppermute x8, starting transfers between devices: 14.3 us -> 11.3 us  [exchange(): out[place] = lax.ppermute(sends[place], axis, pairs)]
    ppermute x8, waiting for transfers between devices: 0.04 us -> 2.53 us  [exchange(): out[place] = lax.ppermute(sends[place], axis, pairs)]
    all_to_all x1, blocking collectives: 12.7 us -> 11.5 us  [one_exchange(): lax.all_to_all(row, ('bx', 'by'), 0, 0)]
    pallas_call x6, Pallas kernels: 9.31 us -> 8.41 us  [call(): pl.pallas_call(kernel, out_shape=[jax.ShapeDtypeStruct(shape, dtype) for...]
  transfers between devices with their start and end apart: 8 -> 8, of which waited for: 0 -> 2; matrix products, arithmetic and copies ran while one was open for 0% -> 0% of each run, Pallas kernels for 12% -> 10%
where the time goes in v1:
time: 34.6 us; the launch traced here: 34.4 us
  blocking collectives  11.5 us (33%)
  starting transfers between devices  11.3 us (33%)
  Pallas kernels  8.41 us (24%)
  waiting for transfers between devices  2.53 us (7%)
  between operations  0.69 us (2%)
    all_to_all x1, blocking collectives, one_exchange(): lax.all_to_all(row, ('bx', 'by'), 0, 0)  11.5 us
    ppermute x8, starting transfers between devices, exchange(): out[place] = lax.ppermute(sends[place], axis, pairs)  11.3 us
    pallas_call x6, Pallas kernels, call(): pl.pallas_call(kernel, out_shape=[jax.ShapeDtypeStruct(shape, dtype) for...  8.41 us
    ppermute x8, waiting for transfers between devices, exchange(): out[place] = lax.ppermute(sends[place], axis, pairs)  2.53 us
  transfers between devices with their start and end apart: 8, of which 2 were waited for; matrix products, arithmetic and copies ran while one was open for 0% of the time, Pallas kernels for 10%

profile of v1, /device:TPU:0, one launch (start us, length us, event | category | flops | bytes accessed | tf_op | source)
XLA Modules:
  0.0 34.4 jit_solution(17253321701876394899)
XLA Ops:
  0.6 1.3 %shard_map.94 = (f32[4,2,2,16,512]{4,3,2,1,0:T(8,128)S(1)}, s32[2,2,16]{2,1,0:T(2,128)S(1)}, f32[2,2,16]{2,1,0:T(2,128)S(1)}, f32[3,8,8]{2,1,0:T(8,128)S(1)}, f3...) custom-call(f32[4,2,2,16,512]{4,3,2,1,0:T(8,128)} %refs_0_.1, ...), custom_call_target="tpu_custom_call" | custom-call | flops 1000000 | bytes 1000000 | tf_op jit(solution)/shard_map/pallas_call | solution.py:842
  1.9 0.6 %collective-permute-start = (f32[16,256]{1,0:T(8,128)S(1)}, f32[16,256]{1,0:T(8,128)S(1)}, u32[]{:S(2)}, u32[]{:S(2)}) collective-permute-start(f32[16,256]{1,0:T(8,128)S(1)} %get-tuple-element.39), channel_id=1, source_target_pairs={{0,4},{8,12},{16,20},{24,28},{4,0},{12,8},{20,16},{28,24},{1,5},{9... | collective-permute-start | bytes 49160 | tf_op jit(solution)/shard_map/ppermute | solution.py:861
  2.5 3.5 %collective-permute-start.1 = (f32[16,256]{1,0:T(8,128)S(1)}, f32[16,256]{1,0:T(8,128)S(1)}, u32[]{:S(2)}, u32[]{:S(2)}) collective-permute-start(f32[16,256]{1,0:T(8,128)S(1)} %get-tuple-element.40), channel_id=1, source_target_pairs={{4,8},{12,16},{20,24},{28,0},{8,4},{16,12},{24,20},{0,28},{5,9},{1... | collective-permute-start | bytes 49160 | tf_op jit(solution)/shard_map/ppermute | solution.py:861
  6.0 1.6 %collective-permute-start.2 = (f32[16,256]{1,0:T(8,128)S(1)}, f32[16,256]{1,0:T(8,128)S(1)}, u32[]{:S(2)}, u32[]{:S(2)}) collective-permute-start(f32[16,256]{1,0:T(8,128)S(1)} %get-tuple-element.41), channel_id=1, source_target_pairs={{0,1},{2,3},{1,0},{3,2},{4,5},{6,7},{5,4},{7,6},{8,9},{10,11},{9,8... | collective-permute-start | bytes 49160 | tf_op jit(solution)/shard_map/ppermute | solution.py:861
  7.6 2.5 %collective-permute-start.3 = (f32[16,256]{1,0:T(8,128)S(1)}, f32[16,256]{1,0:T(8,128)S(1)}, u32[]{:S(2)}, u32[]{:S(2)}) collective-permute-start(f32[16,256]{1,0:T(8,128)S(1)} %get-tuple-element.42), channel_id=1, source_target_pairs={{1,2},{3,0},{2,1},{0,3},{5,6},{7,4},{6,5},{4,7},{9,10},{11,8},{10,... | collective-permute-start | bytes 49160 | tf_op jit(solution)/shard_map/ppermute | solution.py:861
  10.1 1.4 %shard_map.95 = (bf16[512,512]{1,0:T(8,128)(2,1)S(1)}, bf16[128,128]{1,0:T(8,128)(2,1)S(1)}, bf16[128,128]{1,0:T(8,128)(2,1)S(1)}, f32[8,512]{1,0:T(8,128)S(1)},...) custom-call(f32[3,8,8]{2,1,0:T(8,128)S(1)} %get-tuple-element.37.modes_ref, f32[3,8]{1,0:T(4,128)S(1)} %get-tuple-element.36.eigen_ref.refs_3_), custom_call_target="tpu_custom_call" | custom-call | flops 1000000 | bytes 1000000 | tf_op jit(solution)/shard_map/pallas_call | solution.py:842
  11.5 0.0 collective-permute-done.refs_5_.refs_0_
  11.5 0.0 collective-permute-done.1.refs_6_.refs_1_
  11.5 0.0 collective-permute-done.2.refs_7_.refs_2_
  11.5 1.6 %collective-permute-done.3.refs_8_.refs_3_ = f32[16,256]{1,0:T(8,128)S(1)} collective-permute-done((f32[16,256]{1,0:T(8,128)S(1)}, f32[16,256]{1,0:T(8,128)S(1)}, u32[]{:S(2)}, u32[]{:S(2)}) %collective-permute-start.3) | collective-permute-done | bytes 16416 | tf_op jit(solution)/shard_map/ppermute | solution.py:861
  13.2 0.8 %shard_map.96 = (f32[2,2,16,512]{3,2,1,0:T(8,128)S(1)}, f32[8,256]{1,0:T(8,128)S(1)}, f32[8,256]{1,0:T(8,128)S(1)}, f32[8,256]{1,0:T(8,128)S(1)}, f32[8,256]{1,0:T(8,128)S(1)}) custom-call(f32[4,2,2,16,512]{4,3,2,1,0:T(8,128)S(1)} %get-tuple-element.33.refs_0_.basis_ref, f32[2,2,16]{2,1,0:T(2,128)S(1)} %get-tuple-element.34.refs_1_.coef_ref.refs_2_.refs_4_, ...), custom_call_target="tpu_custom_call" | custom-call | flops 1000000 | bytes 1000000 | tf_op jit(solution)/shard_map/pallas_call | solution.py:842
  13.9 0.0 collective-permute-start.4
  14.0 0.6 %collective-permute-start.5 = (f32[8,256]{1,0:T(8,128)S(1)}, f32[8,256]{1,0:T(8,128)S(1)}, u32[]{:S(2)}, u32[]{:S(2)}) collective-permute-start(f32[8,256]{1,0:T(8,128)S(1)} %get-tuple-element.50), channel_id=1, source_target_pairs={{4,8},{12,16},{20,24},{28,0},{8,4},{16,12},{24,20},{0,28},{5,9},{1... | collective-permute-start | bytes 24584 | tf_op jit(solution)/shard_map/ppermute | solution.py:861
  14.6 0.0 collective-permute-start.6
  14.6 2.5 %collective-permute-start.7 = (f32[8,256]{1,0:T(8,128)S(1)}, f32[8,256]{1,0:T(8,128)S(1)}, u32[]{:S(2)}, u32[]{:S(2)}) collective-permute-start(f32[8,256]{1,0:T(8,128)S(1)} %get-tuple-element.52), channel_id=1, source_target_pairs={{1,2},{3,0},{2,1},{0,3},{5,6},{7,4},{6,5},{4,7},{9,10},{11,8},{10,... | collective-permute-start | bytes 24584 | tf_op jit(solution)/shard_map/ppermute | solution.py:861
  17.1 2.1 %shard_map.97 = (f32[8,256]{1,0:T(8,128)S(1)}, f32[16,2,2,16,512]{4,3,2,1,0:T(8,128)S(1)}, f32[2,2,16,512]{3,2,1,0:T(8,128)S(1)}) custom-call(f32[4,2,2,16,512]{4,3,2,1,0:T(8,128)S(1)} %get-tuple-element.33.refs_0_.basis_ref, f32[2,2,16]{2,1,0:T(2,128)S(1)} %get-tuple-element.34.refs_1_.coef_ref.refs_2_.refs_4_, ...), custom_call_target="tpu_custom_call" | custom-call | flops 1000000 | bytes 1000000 | tf_op jit(solution)/shard_map/pallas_call | solution.py:842
  19.2 0.0 collective-permute-done.4.refs_9_
  19.2 0.0 collective-permute-done.5.refs_10_
  19.2 0.0 collective-permute-done.6.refs_11_
  19.2 0.8 %collective-permute-done.7.refs_12_ = f32[8,256]{1,0:T(8,128)S(1)} collective-permute-done((f32[8,256]{1,0:T(8,128)S(1)}, f32[8,256]{1,0:T(8,128)S(1)}, u32[]{:S(2)}, u32[]{:S(2)}) %collective-permute-start.7) | collective-permute-done | bytes 8224 | tf_op jit(solution)/shard_map/ppermute | solution.py:861
  20.1 0.8 %shard_map.98 = (f32[2,2,16,512]{3,2,1,0:T(8,128)S(1)}, f32[192,128]{1,0:T(8,128)S(1)}) custom-call(f32[4,2,2,16,512]{4,3,2,1,0:T(8,128)S(1)} %get-tuple-element.33.refs_0_.basis_ref, f32[2,2,16,512]{3,2,1,0:T(8,128)S(1)} %get-tuple-element.43.refs_1_, f32[2,2,16]{2,1,0:T(2,128)S(1)} %get-tuple-element.34.refs_1_.coef_ref.refs_2_.refs_4_, ...), custom_call_target="tpu_custom_call" | custom-call | flops 1000000 | bytes 1000000 | tf_op jit(solution)/shard_map/pallas_call | solution.py:842
  20.9 11.5 %all_to_all.5 = f32[32,6,1,128]{3,2,1,0:T(1,128)S(1)} all-to-all(f32[32,6,1,128]{3,2,1,0:T(1,128)S(1)} %bitcast.4), channel_id=1, replica_groups=mesh['bx'=8,'by'=4] {'bx','by'}, dimensions={0} | all-to-all | bytes 196608 | tf_op jit(solution)/shard_map/all_to_all | solution.py:919
  32.4 2.0 %shard_map.99 = (f32[2,2,16,512]{3,2,1,0:T(8,128)}, f32[2,2,16,512]{3,2,1,0:T(8,128)}, f32[1,5]{1,0:T(1,128)}) custom-call(f32[4,2,2,16,512]{4,3,2,1,0:T(8,128)S(1)} %get-tuple-element.33.refs_0_.basis_ref, f32[2,2,16,512]{3,2,1,0:T(8,128)S(1)} %get-tuple-element.43.refs_1_, f32[2,2,16,512]{3,2,1,0:T(8,128)S(1)} %get-tuple-element.57.refs_2_, ...), custom_call_target="tpu_custom_call" | custom-call | flops 1000000 | bytes 1000000 | tf_op jit(solution)/shard_map/pallas_call | solution.py:842
Async XLA Ops:
  1.9 9.6 %collective-permute-start = (f32[16,256]{1,0:T(8,128)S(1)}, f32[16,256]{1,0:T(8,128)S(1)}, u32[]{:S(2)}, u32[]{:S(2)}) collective-permute-start(f32[16,256]{1,0:T(8,128)S(1)} %get-tuple-element.39), channel_id=1, source_target_pairs={{0,4},{8,12},{16,20},{24,28},{4,0},{12,8},{20,16},{28,24},{1,5},{9... | collective-permute-start | bytes 49160 | tf_op jit(solution)/shard_map/ppermute | solution.py:861
  2.5 9.0 %collective-permute-start.1 = (f32[16,256]{1,0:T(8,128)S(1)}, f32[16,256]{1,0:T(8,128)S(1)}, u32[]{:S(2)}, u32[]{:S(2)}) collective-permute-start(f32[16,256]{1,0:T(8,128)S(1)} %get-tuple-element.40), channel_id=1, source_target_pairs={{4,8},{12,16},{20,24},{28,0},{8,4},{16,12},{24,20},{0,28},{5,9},{1... | collective-permute-start | bytes 49160 | tf_op jit(solution)/shard_map/ppermute | solution.py:861
  6.0 5.5 %collective-permute-start.2 = (f32[16,256]{1,0:T(8,128)S(1)}, f32[16,256]{1,0:T(8,128)S(1)}, u32[]{:S(2)}, u32[]{:S(2)}) collective-permute-start(f32[16,256]{1,0:T(8,128)S(1)} %get-tuple-element.41), channel_id=1, source_target_pairs={{0,1},{2,3},{1,0},{3,2},{4,5},{6,7},{5,4},{7,6},{8,9},{10,11},{9,8... | collective-permute-start | bytes 49160 | tf_op jit(solution)/shard_map/ppermute | solution.py:861
  7.6 5.5 %collective-permute-start.3 = (f32[16,256]{1,0:T(8,128)S(1)}, f32[16,256]{1,0:T(8,128)S(1)}, u32[]{:S(2)}, u32[]{:S(2)}) collective-permute-start(f32[16,256]{1,0:T(8,128)S(1)} %get-tuple-element.42), channel_id=1, source_target_pairs={{1,2},{3,0},{2,1},{0,3},{5,6},{7,4},{6,5},{4,7},{9,10},{11,8},{10,... | collective-permute-start | bytes 49160 | tf_op jit(solution)/shard_map/ppermute | solution.py:861
  13.9 5.2 %collective-permute-start.4 = (f32[8,256]{1,0:T(8,128)S(1)}, f32[8,256]{1,0:T(8,128)S(1)}, u32[]{:S(2)}, u32[]{:S(2)}) collective-permute-start(f32[8,256]{1,0:T(8,128)S(1)} %get-tuple-element.49), channel_id=1, source_target_pairs={{0,4},{8,12},{16,20},{24,28},{4,0},{12,8},{20,16},{28,24},{1,5},{9... | collective-permute-start | bytes 24584 | tf_op jit(solution)/shard_map/ppermute | solution.py:861
  14.0 5.2 %collective-permute-start.5 = (f32[8,256]{1,0:T(8,128)S(1)}, f32[8,256]{1,0:T(8,128)S(1)}, u32[]{:S(2)}, u32[]{:S(2)}) collective-permute-start(f32[8,256]{1,0:T(8,128)S(1)} %get-tuple-element.50), channel_id=1, source_target_pairs={{4,8},{12,16},{20,24},{28,0},{8,4},{16,12},{24,20},{0,28},{5,9},{1... | collective-permute-start | bytes 24584 | tf_op jit(solution)/shard_map/ppermute | solution.py:861
  14.6 4.6 %collective-permute-start.6 = (f32[8,256]{1,0:T(8,128)S(1)}, f32[8,256]{1,0:T(8,128)S(1)}, u32[]{:S(2)}, u32[]{:S(2)}) collective-permute-start(f32[8,256]{1,0:T(8,128)S(1)} %get-tuple-element.51), channel_id=1, source_target_pairs={{0,1},{2,3},{1,0},{3,2},{4,5},{6,7},{5,4},{7,6},{8,9},{10,11},{9,8... | collective-permute-start | bytes 24584 | tf_op jit(solution)/shard_map/ppermute | solution.py:861
  14.6 5.4 %collective-permute-start.7 = (f32[8,256]{1,0:T(8,128)S(1)}, f32[8,256]{1,0:T(8,128)S(1)}, u32[]{:S(2)}, u32[]{:S(2)}) collective-permute-start(f32[8,256]{1,0:T(8,128)S(1)} %get-tuple-element.52), channel_id=1, source_target_pairs={{1,2},{3,0},{2,1},{0,3},{5,6},{7,4},{6,5},{4,7},{9,10},{11,8},{10,... | collective-permute-start | bytes 24584 | tf_op jit(solution)/shard_map/ppermute | solution.py:861

commit v2 on v1

--- a/solution.py
+++ b/solution.py
@@ -314,25 +314,34 @@
     ids_ref[...] = jnp.broadcast_to(row, (8, LANES))
 
 
+def picker(stride):
+    return lane_ids(PTS, NODES) // stride % PTS == row_ids(PTS, NODES)
+
+
 def expand(matrix, stride):
-    pick = (lane_ids(PTS, NODES) // stride % PTS == row_ids(PTS, NODES)).astype(F32)
-    return jnp.dot(matrix, pick, precision=HIGHEST, preferred_element_type=F32)
-
-
-def tables_kernel(modes_ref, eigen_ref, sb_ref, lh_ref, ll_ref, lx_ref, xy_ref, z_ref):
+    pick = picker(stride).astype(F32).astype(BF16)
+    out, rest = None, matrix
+    for _ in range(3):
+        part = rest.astype(BF16)
+        rest = rest - part.astype(F32)
+        term = jnp.dot(part, pick, preferred_element_type=F32)
+        out = term if out is None else out + term
+    return out
+
+
+def tables_kernel(scale, modes_ref, eigen_ref, basis_ref, coef_ref, mask_ref, *refs):
+    sb_ref, lh_ref, ll_ref, lx_ref, xy_ref, z_ref, extended_ref, divisor_ref, sums_ref = refs
     strides = (PTS * PTS, PTS, 1)
-    eye = (row_ids(PTS, PTS) == lane_ids(PTS, PTS)).astype(F32)
     straight, stiff, unit = [], [], []
     for d in range(3):
         mode = modes_ref[d]
-        turn = lax.dot_general(
-            mode, eye, (((0,), (0,)), ((), ())), precision=HIGHEST, preferred_element_type=F32
+        scaled = mode * eigen_ref[d : d + 1, :]
+        one = lax.dot_general(
+            scaled, mode, (((1,), (1,)), ((), ())), precision=HIGHEST, preferred_element_type=F32
         )
-        scaled = mode * eigen_ref[d : d + 1, :]
-        one = jnp.dot(scaled, turn, precision=HIGHEST, preferred_element_type=F32)
         straight.append(expand(mode, strides[d]))
         stiff.append(expand(one, strides[d]))
-        unit.append(expand(eye, strides[d]))
+        unit.append(picker(strides[d]).astype(F32))
     for i in range(PTS):
         for j in range(PTS):
             rows = slice((i * PTS + j) * PTS, (i * PTS + j + 1) * PTS)
@@ -380,34 +389,55 @@
         z_ref[(CGZ + level) * EZ : (CGZ + level + 1) * EZ, :] = jnp.dot(
             tall, stiff[2], precision=HIGHEST, preferred_element_type=F32
         )
-
-
-def spectrum_row(eigen_ref):
-    out = jnp.zeros((1, NODES), F32)
-    for d, stride in enumerate((PTS * PTS, PTS, 1)):
-        pick = (lane_ids(PTS, NODES) // stride % PTS == row_ids(PTS, NODES)).astype(F32)
-        out = out + jnp.dot(
-            eigen_ref[d : d + 1, :], pick, precision=HIGHEST, preferred_element_type=F32
-        )
-    return out
+    spectrum = functools.reduce(
+        jnp.add, [expand(eigen_ref[d : d + 1, :], strides[d]) for d in range(3)]
+    )
+    current = load_groups(basis_ref, KV - 1)
+    inside = own_neighbors(current)
+    coef = columns(coef_ref)
+    for x in range(EX):
+        for y in range(EY):
+            extended_ref[x, y] = current[x][y] + inside[x][y]
+            divisor_ref[x, y] = coef[x][y] * spectrum + SHIFT
+    sums_ref[...] = jnp.zeros_like(sums_ref)
+    halves = range(EZ // HALF)
+
+    def vectors(half):
+        return {v: (lambda x, y, r, c, v=v: basis_ref[v, x, y, r, c]) for v in range(KV)}
+
+    def put(row, value):
+        sums_ref[row : row + 1, :] = value
+
+    position = {}
+    for v in range(KV):
+        for u in range(v, KV):
+            position[v, u] = len(position)
+    products(vectors, lambda half: None, halves, lambda v, u, s: put(AT_GRAM + position[v, u], s))
+    for level in range(CGZ):
+        sums = [[None] * EY for _ in range(EX)]
+        for x in range(EX):
+            for y in range(EY):
+                sums[x][y] = fold(current[x][y] * z_ref[level * EZ : (level + 1) * EZ, :])
+        for ab in range(4):
+            total = jnp.zeros((1, NODES), F32)
+            for x in range(EX):
+                for y in range(EY):
+                    at = (ab * EX + x) * EY + y
+                    total = total + sums[x][y] * xy_ref[at : at + 1, :]
+            parts = [total[:, c : c + LANES] for c in range(0, NODES, LANES)]
+            put(AT_SUM + ab * CGZ + level, functools.reduce(jnp.add, parts) * scale)
 
 
 def smooth_kernel(*refs):
-    basis_ref, coef_ref, mask_ref, eigen_ref, sb_ref = refs[:5]
-    halo = [ref[0:8, :] for ref in refs[5:9]]
-    smooth_ref, *send = refs[9:]
-    current = load_groups(basis_ref, KV - 1)
-    inside, outside = own_neighbors(current), unpack_all(halo)
-    coef, active = columns(coef_ref), columns(mask_ref)
-    extended = [
-        [current[x][y] + (inside[x][y] + outside[x][y]) for y in range(EY)] for x in range(EX)
-    ]
+    own_ref, divisor_ref, mask_ref, sb_ref = refs[:4]
+    halo = [ref[0:8, :] for ref in refs[4:8]]
+    smooth_ref, *send = refs[8:]
+    own, outside = load_groups(own_ref), unpack_all(halo)
+    active = columns(mask_ref)
+    extended = [[own[x][y] + outside[x][y] for y in range(EY)] for x in range(EX)]
     modal = jnp.dot(stack(extended).astype(BF16), sb_ref[...], preferred_element_type=F32)
     modal = unstack(modal)
-    spectrum = spectrum_row(eigen_ref)
-    modal = [
-        [modal[x][y] / (coef[x][y] * spectrum + SHIFT) for y in range(EY)] for x in range(EX)
-    ]
+    modal = [[modal[x][y] / divisor_ref[x, y] for y in range(EY)] for x in range(EX)]
     smooth = lax.dot_general(
         stack(modal).astype(BF16),
         sb_ref[...],
@@ -576,19 +606,27 @@
         out_row(v, w, fold(acc))
 
 
-def fields_kernel(scale, basis_ref, coef_ref, mask_ref, *refs):
+def fields_kernel(basis_ref, coef_ref, mask_ref, *refs):
     mask_refs, (xy_ref, z_ref) = refs[:4], refs[4:6]
-    early_ref, field_ref, wall_ref, rows_ref = refs[6:]
+    smooth_ref, lh_ref, ll_ref, lx_ref, sums_ref = refs[6:11]
+    early_ref, field_ref, wall_ref, part_ref, rows_ref = refs[11:]
     coef, active = columns(coef_ref), columns(mask_ref)
     wide = [[jnp.broadcast_to(active[x][y], (EZ, NODES)) for y in range(EY)] for x in range(EX)]
     inside, outside = own_neighbors(wide), unpack_all([ref[8:16, :] for ref in mask_refs])
     counts = face_count(EZ)
     halves = range(EZ // HALF)
     levels = [levels_of(half) for half in halves]
+    smooth = load_groups(smooth_ref)
+    stiff_part = stiff_apply(smooth, lh_ref, ll_ref, lx_ref)
+    inside_part = own_neighbors(smooth)
     for x in range(EX):
         for y in range(EY):
             wall = active[x][y] * PENALTY * (counts - (inside[x][y] + outside[x][y]))
             wall_ref[x, y] = wall
+            part_ref[x, y] = active[x][y] * (
+                coef[x][y] * stiff_part[x][y]
+                + PENALTY * (counts * smooth[x][y] - inside_part[x][y])
+            )
             weight = active[x][y] * coef[x][y]
             for half in halves:
                 rows = slice(half * HALF, half * HALF + HALF)
@@ -603,7 +641,8 @@
                         field_ref[ab * CGZ + level, x, y, rows, :] = (
                             z_ref[tall, :] * first + z_ref[stiff, :] * second
                         )
-    rows_ref[...] = jnp.zeros_like(rows_ref)
+    rows_ref[:LANES, :] = jnp.zeros((LANES, LANES), F32)
+    rows_ref[LANES:, :] = sums_ref[...]
 
     def fields(ab):
         def at(half):
@@ -620,56 +659,29 @@
     def put(row, value):
         rows_ref[row : row + 1, :] = value
 
-    position = {}
-    for v in range(KV):
-        for u in range(v, KV):
-            position[v, u] = len(position)
-
     def put_field(v, w, value):
         far = (w - v) % VERTS
         if far > VERTS // 2 or (far == VERTS // 2 and v > w):
             v, far = w, VERTS - far
         put(LANES + AT_FAR + v if far == VERTS // 2 else far * VERTS + v, value)
 
-    products(vectors, lambda half: None, halves, lambda v, u, s: put(LANES + AT_GRAM + position[v, u], s))
     for ab in range(4):
         products(vectors, fields(ab), halves, lambda v, w, s: put(LANES + v * VERTS + w, s))
         products(fields(ab), lambda half: None, halves, put_field)
         for other in range(ab + 1, 4):
             products(fields(ab), fields(other), halves, put_field)
-    for level in range(CGZ):
-        sums = [[None] * EY for _ in range(EX)]
-        for x in range(EX):
-            for y in range(EY):
-                sums[x][y] = fold(basis_ref[KV - 1, x, y] * z_ref[level * EZ : (level + 1) * EZ, :])
-        for ab in range(4):
-            total = jnp.zeros((1, NODES), F32)
-            for x in range(EX):
-                for y in range(EY):
-                    at = (ab * EX + x) * EY + y
-                    total = total + sums[x][y] * xy_ref[at : at + 1, :]
-            parts = [total[:, c : c + LANES] for c in range(0, NODES, LANES)]
-            put(LANES + AT_SUM + ab * CGZ + level, functools.reduce(jnp.add, parts) * scale)
     early_ref[...] = lane_sums(rows_ref[...])
 
 
 def base_kernel(rows, peers, *refs):
-    basis_ref, smooth_ref, coef_ref, mask_ref, ids_ref, inverse_ref = refs[:6]
-    lh_ref, ll_ref, lx_ref = refs[6:9]
-    face_refs, early_ref, field_ref = refs[9:13], refs[13], refs[14]
-    base_ref, send_ref, rows_ref = refs[15:]
-    coef, active = columns(coef_ref), columns(mask_ref)
-    smooth = load_groups(smooth_ref)
-    stiff = stiff_apply(smooth, lh_ref, ll_ref, lx_ref)
-    inside = own_neighbors(smooth)
+    basis_ref, part_ref, mask_ref, ids_ref, inverse_ref = refs[:5]
+    face_refs, early_ref, field_ref = refs[5:9], refs[9], refs[10]
+    base_ref, send_ref, rows_ref = refs[11:]
+    active = columns(mask_ref)
     outside = unpack_all([ref[...] for ref in face_refs])
-    counts = face_count(EZ)
     for x in range(EX):
         for y in range(EY):
-            base_ref[x, y] = active[x][y] * (
-                coef[x][y] * stiff[x][y]
-                + PENALTY * (counts * smooth[x][y] - (inside[x][y] + outside[x][y]))
-            )
+            base_ref[x, y] = part_ref[x, y] - (PENALTY * active[x][y]) * outside[x][y]
     rows_ref[...] = jnp.zeros_like(rows_ref)
     halves = range(EZ // HALF)
 
@@ -712,8 +724,8 @@
 
 def close_kernel(total_points, rows, peers, *refs):
     basis_ref, smooth_ref, base_ref, wall_ref, coef_ref, mask_ref = refs[:6]
-    xy_ref, z_ref, got_ref, precond_hbm, next_hbm, hessen_ref = refs[6:12]
-    precond_ref, next_ref, sems = refs[12:]
+    xy_ref, z_ref, got_ref, precond_hbm, next_hbm, hessen_hbm = refs[6:12]
+    precond_ref, next_ref, hessen_ref, sems = refs[12:]
     lane, row = lane_ids(peers, LANES), row_ids(peers, LANES)
     side = lax.axis_size("by")
 
@@ -809,6 +821,12 @@
     gram = jnp.sum(pair * plain, axis=1, keepdims=True) / total_points
     dot = functools.reduce(jnp.add, [p * p for p in proj])
     beta = jnp.sqrt(square - 2.0 * dot + gram + EPSILON)
+    result = jnp.zeros((1, LANES), F32)
+    for v, value in enumerate(proj + [beta]):
+        result = jnp.where(line == v, value, result)
+    hessen_ref[...] = result[:, : KV + 1]
+    copies.append(pltpu.make_async_copy(hessen_ref, hessen_hbm, sems.at[2 * EX * EY]))
+    copies[-1].start()
     inverse = 1.0 / beta
     for x in range(EX):
         for y in range(EY):
@@ -823,13 +841,9 @@
             for v in range(KV):
                 residual = residual - proj[v] * basis_ref[v, x, y]
             next_ref[x, y] = residual * inverse
-            n = len(copies)
+            n = EX * EY + x * EY + y
             copies.append(pltpu.make_async_copy(next_ref.at[x, y], next_hbm.at[x, y], sems.at[n]))
             copies[-1].start()
-    result = jnp.zeros((1, LANES), F32)
-    for v, value in enumerate(proj + [beta]):
-        result = jnp.where(line == v, value, result)
-    hessen_ref[...] = result[:, : KV + 1]
     for copy in copies:
         copy.wait()
 
@@ -864,20 +878,20 @@
 
 def smooth_part(basis, coef, modes, eigen, mask, sends):
     halo = exchange(sends)
-    square = ((NODES, NODES), BF16)
     tables = call(
-        tables_kernel,
-        [square]
+        functools.partial(tables_kernel, 1.0 / math.sqrt(EX * EY * EZ * NODES)),
+        [((NODES, NODES), BF16)]
         + [((LANES, LANES), BF16)] * 2
-        + [((8, NODES), F32), ((2 * XY, NODES), F32), ((2 * CGZ * EZ, NODES), F32)],
-        [spec()] * 2,
-        (modes, eigen),
+        + [((8, NODES), F32), ((2 * XY, NODES), F32), ((2 * CGZ * EZ, NODES), F32)]
+        + [FIELD, FIELD, ((LANES, LANES), F32)],
+        [spec()] * 5,
+        (modes, eigen, basis, coef, mask),
     )
     smooth, *sends = call(
         smooth_kernel,
         [FIELD] + [((8, 256), F32)] * 4,
-        [spec()] * 9,
-        (basis, coef, mask, eigen, tables[0], *halo),
+        [spec()] * 8,
+        (tables[6], tables[7], mask, tables[0], *halo),
     )
     return halo, tables, smooth, exchange(sends)
 
@@ -901,18 +915,18 @@
     )
     basis, mask, coef, modes, eigen, coarse_inverse, ids = local
     halo, tables, smooth, faces = smooth_part(basis, coef, modes, eigen, mask, (a, b, c, d))
-    early, fields, wall = call(
-        functools.partial(fields_kernel, 1.0 / math.sqrt(points)),
-        [((8, 2 * LANES), F32), ((VERTS,) + FIELD[0], F32), FIELD],
-        [spec()] * 9,
-        (basis, coef, mask, *halo, tables[4], tables[5]),
+    early, fields, wall, part = call(
+        fields_kernel,
+        [((8, 2 * LANES), F32), ((VERTS,) + FIELD[0], F32), FIELD, FIELD],
+        [spec()] * 14,
+        (basis, coef, mask, *halo, tables[4], tables[5], smooth, *tables[1:4], tables[8]),
         scratch=[pltpu.VMEM((2 * LANES, LANES), F32)],
     )
     base, row = call(
         functools.partial(base_kernel, rows, peers),
         [FIELD, (((SENT + rows) * peers, LANES), F32)],
-        [spec()] * 15,
-        (basis, smooth, coef, mask, ids, coarse_inverse, *tables[1:4], *faces, early, fields),
+        [spec()] * 11,
+        (basis, part, mask, ids, coarse_inverse, *faces, early, fields),
         scratch=[pltpu.VMEM((LANES, LANES), F32)],
     )
     row = row.reshape(peers, SENT + rows, 1, LANES)
@@ -922,8 +936,9 @@
         [FIELD, FIELD, ((1, KV + 1), F32)],
         [spec()] * 9,
         (basis, smooth, base, wall, coef, mask, tables[4], tables[5], got),
-        out_specs=[spec(pltpu.HBM), spec(pltpu.HBM), spec()],
-        scratch=[pltpu.VMEM(*FIELD), pltpu.VMEM(*FIELD), pltpu.SemaphoreType.DMA((2 * EX * EY,))],
+        out_specs=[spec(pltpu.HBM)] * 3,
+        scratch=[pltpu.VMEM(*FIELD)] * 2
+        + [pltpu.VMEM((1, KV + 1), F32), pltpu.SemaphoreType.DMA((2 * EX * EY + 1,))],
     )
     return precond, next_vector, hessen.reshape(KV + 1)
 

time: 34.6 us -> 33.6 us (0.971)
  Pallas kernels: 8.41 us -> 7.43 us
    pallas_call x6, Pallas kernels: 8.41 us -> 7.43 us  [call(): pl.pallas_call(kernel, out_shape=[jax.ShapeDtypeStruct(shape, dtype) for...]
where the time goes in v2:
time: 33.6 us; the launch traced here: 33.4 us
  blocking collectives  11.5 us (34%)
  starting transfers between devices  11.3 us (34%)
  Pallas kernels  7.43 us (22%)
  waiting for transfers between devices  2.5 us (7%)
  between operations  0.71 us (2%)
    all_to_all x1, blocking collectives, one_exchange(): lax.all_to_all(row, ('bx', 'by'), 0, 0)  11.5 us
    ppermute x8, starting transfers between devices, exchange(): out[place] = lax.ppermute(sends[place], axis, pairs)  11.3 us
    pallas_call x6, Pallas kernels, call(): pl.pallas_call(kernel, out_shape=[jax.ShapeDtypeStruct(shape, dtype) for...  7.43 us
    ppermute x8, waiting for transfers between devices, exchange(): out[place] = lax.ppermute(sends[place], axis, pairs)  2.5 us
  transfers between devices with their start and end apart: 8, of which 2 were waited for; matrix products, arithmetic and copies ran while one was open for 0% of the time, Pallas kernels for 10%

profile of v2, /device:TPU:0, one launch (start us, length us, event | category | flops | bytes accessed | tf_op | source)
XLA Modules:
  0.0 33.4 jit_solution(7784139498629124320)
XLA Ops:
  0.6 1.3 %shard_map.94 = (f32[4,2,2,16,512]{4,3,2,1,0:T(8,128)S(1)}, s32[2,2,16]{2,1,0:T(2,128)S(1)}, f32[2,2,16]{2,1,0:T(2,128)S(1)}, f32[3,8,8]{2,1,0:T(8,128)S(1)}, f3...) custom-call(f32[4,2,2,16,512]{4,3,2,1,0:T(8,128)} %refs_0_.1, ...), custom_call_target="tpu_custom_call" | custom-call | flops 1000000 | bytes 1000000 | tf_op jit(solution)/shard_map/pallas_call | solution.py:856
  1.9 0.6 %collective-permute-start = (f32[16,256]{1,0:T(8,128)S(1)}, f32[16,256]{1,0:T(8,128)S(1)}, u32[]{:S(2)}, u32[]{:S(2)}) collective-permute-start(f32[16,256]{1,0:T(8,128)S(1)} %get-tuple-element.45), channel_id=1, source_target_pairs={{0,4},{8,12},{16,20},{24,28},{4,0},{12,8},{20,16},{28,24},{1,5},{9... | collective-permute-start | bytes 49160 | tf_op jit(solution)/shard_map/ppermute | solution.py:875
  2.5 3.5 %collective-permute-start.1 = (f32[16,256]{1,0:T(8,128)S(1)}, f32[16,256]{1,0:T(8,128)S(1)}, u32[]{:S(2)}, u32[]{:S(2)}) collective-permute-start(f32[16,256]{1,0:T(8,128)S(1)} %get-tuple-element.46), channel_id=1, source_target_pairs={{4,8},{12,16},{20,24},{28,0},{8,4},{16,12},{24,20},{0,28},{5,9},{1... | collective-permute-start | bytes 49160 | tf_op jit(solution)/shard_map/ppermute | solution.py:875
  6.0 1.6 %collective-permute-start.2 = (f32[16,256]{1,0:T(8,128)S(1)}, f32[16,256]{1,0:T(8,128)S(1)}, u32[]{:S(2)}, u32[]{:S(2)}) collective-permute-start(f32[16,256]{1,0:T(8,128)S(1)} %get-tuple-element.47), channel_id=1, source_target_pairs={{0,1},{2,3},{1,0},{3,2},{4,5},{6,7},{5,4},{7,6},{8,9},{10,11},{9,8... | collective-permute-start | bytes 49160 | tf_op jit(solution)/shard_map/ppermute | solution.py:875
  7.6 2.5 %collective-permute-start.3 = (f32[16,256]{1,0:T(8,128)S(1)}, f32[16,256]{1,0:T(8,128)S(1)}, u32[]{:S(2)}, u32[]{:S(2)}) collective-permute-start(f32[16,256]{1,0:T(8,128)S(1)} %get-tuple-element.48), channel_id=1, source_target_pairs={{1,2},{3,0},{2,1},{0,3},{5,6},{7,4},{6,5},{4,7},{9,10},{11,8},{10,... | collective-permute-start | bytes 49160 | tf_op jit(solution)/shard_map/ppermute | solution.py:875
  10.1 1.3 %shard_map.95 = (bf16[512,512]{1,0:T(8,128)(2,1)S(1)}, bf16[128,128]{1,0:T(8,128)(2,1)S(1)}, bf16[128,128]{1,0:T(8,128)(2,1)S(1)}, f32[8,512]{1,0:T(8,128)S(1)},...) custom-call(f32[3,8,8]{2,1,0:T(8,128)S(1)} %get-tuple-element.38.mod, ...), custom_call_target="tpu_custom_call" | custom-call | flops 1000000 | bytes 1000000 | tf_op jit(solution)/shard_map/pallas_call | solution.py:856
  11.4 0.0 collective-permute-done.refs_4_.refs_0_
  11.4 0.0 collective-permute-done.1.refs_5_.refs_1_
  11.4 0.0 collective-permute-done.2.refs_6_.refs_2_
  11.4 1.7 %collective-permute-done.3.refs_7_.refs_3_ = f32[16,256]{1,0:T(8,128)S(1)} collective-permute-done((f32[16,256]{1,0:T(8,128)S(1)}, f32[16,256]{1,0:T(8,128)S(1)}, u32[]{:S(2)}, u32[]{:S(2)}) %collective-permute-start.3) | collective-permute-done | bytes 16416 | tf_op jit(solution)/shard_map/ppermute | solution.py:875
  13.2 0.6 %shard_map.96 = (f32[2,2,16,512]{3,2,1,0:T(8,128)S(1)}, f32[8,256]{1,0:T(8,128)S(1)}, f32[8,256]{1,0:T(8,128)S(1)}, f32[8,256]{1,0:T(8,128)S(1)}, f32[8,256]{1,0:T(8,128)S(1)}) custom-call(f32[2,2,16,512]{3,2,1,0:T(8,128)S(1)} %get-tuple-element.42.refs_0_, f32[2,2,16,512]{3,2,1,0:T(8,128)S(1)} %get-tuple-element.43.refs_1_, ...), custom_call_target="tpu_custom_call" | custom-call | flops 1000000 | bytes 1000000 | tf_op jit(solution)/shard_map/pallas_call | solution.py:856
  13.7 0.0 collective-permute-start.4
  13.8 0.6 %collective-permute-start.5 = (f32[8,256]{1,0:T(8,128)S(1)}, f32[8,256]{1,0:T(8,128)S(1)}, u32[]{:S(2)}, u32[]{:S(2)}) collective-permute-start(f32[8,256]{1,0:T(8,128)S(1)} %get-tuple-element.60), channel_id=1, source_target_pairs={{4,8},{12,16},{20,24},{28,0},{8,4},{16,12},{24,20},{0,28},{5,9},{1... | collective-permute-start | bytes 24584 | tf_op jit(solution)/shard_map/ppermute | solution.py:875
  14.4 0.0 collective-permute-start.6
  14.4 2.5 %collective-permute-start.7 = (f32[8,256]{1,0:T(8,128)S(1)}, f32[8,256]{1,0:T(8,128)S(1)}, u32[]{:S(2)}, u32[]{:S(2)}) collective-permute-start(f32[8,256]{1,0:T(8,128)S(1)} %get-tuple-element.62), channel_id=1, source_target_pairs={{1,2},{3,0},{2,1},{0,3},{5,6},{7,4},{6,5},{4,7},{9,10},{11,8},{10,... | collective-permute-start | bytes 24584 | tf_op jit(solution)/shard_map/ppermute | solution.py:875
  16.9 2.2 %shard_map.97 = (f32[8,256]{1,0:T(8,128)S(1)}, f32[16,2,2,16,512]{4,3,2,1,0:T(8,128)S(1)}, f32[2,2,16,512]{3,2,1,0:T(8,128)S(1)}, f32[2,2,16,512]{3,2,1,0:T(8,128)S(1)}) custom-call(f32[4,2,2,16,512]{4,3,2,1,0:T(8,128)S(1)} %get-tuple-element.37.basis_ref.refs_0_, f32[2,2,16]{2,1,0:T(2,128)S(1)} %get-tuple-element.40.coef_ref.refs_4_, ...), custom_call_target="tpu_custom_call" | custom-call | flops 1000000 | bytes 1000000 | tf_op jit(solution)/shard_map/pallas_call | solution.py:856
  19.1 0.0 collective-permute-done.4.refs_5_
  19.1 0.0 collective-permute-done.5.refs_6_
  19.2 0.0 collective-permute-done.6.refs_7_
  19.2 0.7 %collective-permute-done.7.refs_8_ = f32[8,256]{1,0:T(8,128)S(1)} collective-permute-done((f32[8,256]{1,0:T(8,128)S(1)}, f32[8,256]{1,0:T(8,128)S(1)}, u32[]{:S(2)}, u32[]{:S(2)}) %collective-permute-start.7) | collective-permute-done | bytes 8224 | tf_op jit(solution)/shard_map/ppermute | solution.py:875
  19.9 0.5 %shard_map.98 = (f32[2,2,16,512]{3,2,1,0:T(8,128)S(1)}, f32[192,128]{1,0:T(8,128)S(1)}) custom-call(f32[4,2,2,16,512]{4,3,2,1,0:T(8,128)S(1)} %get-tuple-element.37.basis_ref.refs_0_, f32[2,2,16,512]{3,2,1,0:T(8,128)S(1)} %get-tuple-element.56.refs_1_, s32[2,2,16]{2,1,0:T(2,128)S(1)} %get-tuple-element.41.mask_ref.refs_2_.refs_5_, ...), custom_call_target="tpu_custom_call" | custom-call | flops 1000000 | bytes 1000000 | tf_op jit(solution)/shard_map/pallas_call | solution.py:856
  20.4 11.5 %all_to_all.5 = f32[32,6,1,128]{3,2,1,0:T(1,128)S(1)} all-to-all(f32[32,6,1,128]{3,2,1,0:T(1,128)S(1)} %bitcast.4), channel_id=1, replica_groups=mesh['bx'=8,'by'=4] {'bx','by'}, dimensions={0} | all-to-all | bytes 196608 | tf_op jit(solution)/shard_map/all_to_all | solution.py:933
  31.9 1.6 %shard_map.99 = (f32[2,2,16,512]{3,2,1,0:T(8,128)}, f32[2,2,16,512]{3,2,1,0:T(8,128)}, f32[1,5]{1,0:T(1,128)}) custom-call(f32[4,2,2,16,512]{4,3,2,1,0:T(8,128)S(1)} %get-tuple-element.37.basis_ref.refs_0_, f32[2,2,16,512]{3,2,1,0:T(8,128)S(1)} %get-tuple-element.49.refs_6_.refs_1_, f32[2,2,16,512]{3,2,1,0:T(8,128)S(1)} %get-tuple-element.65.refs_2_, ...), custom_call_target="tpu_custom_call" | custom-call | flops 1000000 | bytes 1000000 | tf_op jit(solution)/shard_map/pallas_call | solution.py:856
Async XLA Ops:
  1.9 9.4 %collective-permute-start = (f32[16,256]{1,0:T(8,128)S(1)}, f32[16,256]{1,0:T(8,128)S(1)}, u32[]{:S(2)}, u32[]{:S(2)}) collective-permute-start(f32[16,256]{1,0:T(8,128)S(1)} %get-tuple-element.45), channel_id=1, source_target_pairs={{0,4},{8,12},{16,20},{24,28},{4,0},{12,8},{20,16},{28,24},{1,5},{9... | collective-permute-start | bytes 49160 | tf_op jit(solution)/shard_map/ppermute | solution.py:875
  2.5 8.9 %collective-permute-start.1 = (f32[16,256]{1,0:T(8,128)S(1)}, f32[16,256]{1,0:T(8,128)S(1)}, u32[]{:S(2)}, u32[]{:S(2)}) collective-permute-start(f32[16,256]{1,0:T(8,128)S(1)} %get-tuple-element.46), channel_id=1, source_target_pairs={{4,8},{12,16},{20,24},{28,0},{8,4},{16,12},{24,20},{0,28},{5,9},{1... | collective-permute-start | bytes 49160 | tf_op jit(solution)/shard_map/ppermute | solution.py:875
  6.0 5.4 %collective-permute-start.2 = (f32[16,256]{1,0:T(8,128)S(1)}, f32[16,256]{1,0:T(8,128)S(1)}, u32[]{:S(2)}, u32[]{:S(2)}) collective-permute-start(f32[16,256]{1,0:T(8,128)S(1)} %get-tuple-element.47), channel_id=1, source_target_pairs={{0,1},{2,3},{1,0},{3,2},{4,5},{6,7},{5,4},{7,6},{8,9},{10,11},{9,8... | collective-permute-start | bytes 49160 | tf_op jit(solution)/shard_map/ppermute | solution.py:875
  7.6 5.5 %collective-permute-start.3 = (f32[16,256]{1,0:T(8,128)S(1)}, f32[16,256]{1,0:T(8,128)S(1)}, u32[]{:S(2)}, u32[]{:S(2)}) collective-permute-start(f32[16,256]{1,0:T(8,128)S(1)} %get-tuple-element.48), channel_id=1, source_target_pairs={{1,2},{3,0},{2,1},{0,3},{5,6},{7,4},{6,5},{4,7},{9,10},{11,8},{10,... | collective-permute-start | bytes 49160 | tf_op jit(solution)/shard_map/ppermute | solution.py:875
  13.7 5.4 %collective-permute-start.4 = (f32[8,256]{1,0:T(8,128)S(1)}, f32[8,256]{1,0:T(8,128)S(1)}, u32[]{:S(2)}, u32[]{:S(2)}) collective-permute-start(f32[8,256]{1,0:T(8,128)S(1)} %get-tuple-element.59), channel_id=1, source_target_pairs={{0,4},{8,12},{16,20},{24,28},{4,0},{12,8},{20,16},{28,24},{1,5},{9... | collective-permute-start | bytes 24584 | tf_op jit(solution)/shard_map/ppermute | solution.py:875
  13.8 5.4 %collective-permute-start.5 = (f32[8,256]{1,0:T(8,128)S(1)}, f32[8,256]{1,0:T(8,128)S(1)}, u32[]{:S(2)}, u32[]{:S(2)}) collective-permute-start(f32[8,256]{1,0:T(8,128)S(1)} %get-tuple-element.60), channel_id=1, source_target_pairs={{4,8},{12,16},{20,24},{28,0},{8,4},{16,12},{24,20},{0,28},{5,9},{1... | collective-permute-start | bytes 24584 | tf_op jit(solution)/shard_map/ppermute | solution.py:875
  14.4 4.8 %collective-permute-start.6 = (f32[8,256]{1,0:T(8,128)S(1)}, f32[8,256]{1,0:T(8,128)S(1)}, u32[]{:S(2)}, u32[]{:S(2)}) collective-permute-start(f32[8,256]{1,0:T(8,128)S(1)} %get-tuple-element.61), channel_id=1, source_target_pairs={{0,1},{2,3},{1,0},{3,2},{4,5},{6,7},{5,4},{7,6},{8,9},{10,11},{9,8... | collective-permute-start | bytes 24584 | tf_op jit(solution)/shard_map/ppermute | solution.py:875
  14.4 5.4 %collective-permute-start.7 = (f32[8,256]{1,0:T(8,128)S(1)}, f32[8,256]{1,0:T(8,128)S(1)}, u32[]{:S(2)}, u32[]{:S(2)}) collective-permute-start(f32[8,256]{1,0:T(8,128)S(1)} %get-tuple-element.62), channel_id=1, source_target_pairs={{1,2},{3,0},{2,1},{0,3},{5,6},{7,4},{6,5},{4,7},{9,10},{11,8},{10,... | collective-permute-start | bytes 24584 | tf_op jit(solution)/shard_map/ppermute | solution.py:875
